TPU v7x, 256 devices: a whole 4x4x8 slice. The times are simulated.
256 devices in a mesh: frames: 8 (over y, x_lo), labels: 8 (over z), hidden: 4 (over x_hi, core).
Axes of the slice: x: 4 (x_hi: 2, x_lo: 2; x = x_hi * 2 + x_lo), y: 4, z: 8, core: 2. Of those that a mesh axis runs over, the one named last changes fastest.
Arguments:
- features: bfloat16 [1024, 1024], P('frames'), may hold values from -6 to 6
- up_weight: bfloat16 [1024, 4096], P(None, 'hidden'), may hold values from -0.1875 to 0.1875
- down_weight: bfloat16 [4096, 640], P('hidden'), may hold values from -0.09375 to 0.09375
- predictor: bfloat16 [512, 640], P(('labels', 'hidden')), may hold values from -4 to 4
- out_weight: bfloat16 [640, 1024], replicated, may hold values from -1.1 to 1.1
- blank_weight: float32 [1024, 512], P('frames', ('labels', 'hidden')), may hold values from 0 to 0.06
- label_weight: float32 [1024, 512], P('frames', ('labels', 'hidden')), may hold values from 0 to 0.06
- targets: int32 [512], P(('labels', 'hidden')), may hold values from 1 to 1023
Outputs:
- enc_grad: float32 [1024, 640], P(('frames', 'labels', 'hidden'))
- pred_grad: float32 [512, 640], P(('labels', 'hidden'))
- head_grad: float32 [1024, 640], P(('frames', 'labels', 'hidden'))
All inputs are finite; a program needn't handle non-finite values.
Results may differ from a plain program's by a relative error of at most 0.0023.
Values sent between devices are 32-bit elements; how exact they have to be, the bound alone decides.
A program may use at most 64 MiB of HBM per device.

v0:
```python
import math

import jax
import jax.numpy as jnp
from jax import lax
from jax.sharding import PartitionSpec as P


def on_device(
    features, up_weight, down_weight, predictor, out_weight, blank_weight, label_weight, targets
):
    frames_dev = features.shape[0]
    labels_dev = predictor.shape[0]
    joint_width = predictor.shape[1]
    vocab_size = out_weight.shape[1]
    hidden_act = jax.nn.relu(
        jnp.dot(features, up_weight, preferred_element_type=jnp.float32)
    ).astype(jnp.bfloat16)
    partial_enc = jnp.dot(hidden_act, down_weight, preferred_element_type=jnp.float32)
    encoded = lax.psum(partial_enc, "hidden")
    block_rows = min(frames_dev, max(1, 512 // labels_dev))
    while frames_dev % block_rows:
        block_rows = block_rows - 1
    pred_wide = predictor.astype(jnp.float32)
    vocab_ids = jnp.arange(vocab_size, dtype=jnp.int32)
    label_hot = (targets[:, None] == vocab_ids[None, :]).astype(jnp.float32)
    blank_hot = (vocab_ids == 0).astype(jnp.float32)
    cell_hot = jnp.broadcast_to(label_hot[None], (block_rows, labels_dev, vocab_size)).reshape(
        -1, vocab_size
    )

    def joint_step(pred_sum, inputs):
        enc_block, blank_block, label_block = inputs
        joint_cells = jnp.tanh(enc_block[:, None, :] + pred_wide[None, :, :]).astype(jnp.bfloat16)
        joint_cells = joint_cells.reshape(block_rows * labels_dev, joint_width)
        logits = jnp.dot(joint_cells, out_weight, preferred_element_type=jnp.float32)
        top_logit = jnp.max(logits, axis=1, keepdims=True)
        log_total = top_logit + jnp.log(jnp.sum(jnp.exp(logits - top_logit), axis=1, keepdims=True))
        probs = jnp.exp(logits - log_total)
        blank_flat = blank_block.reshape(-1, 1)
        label_flat = label_block.reshape(-1, 1)
        logit_grad = (
            (blank_flat + label_flat) * probs - blank_flat * blank_hot - label_flat * cell_hot
        ).astype(jnp.bfloat16)
        joint_grad = lax.dot_general(
            logit_grad, out_weight, (((1,), (1,)), ((), ())), preferred_element_type=jnp.float32
        )
        cells_wide = joint_cells.astype(jnp.float32)
        tanh_grad = (joint_grad * (1.0 - cells_wide * cells_wide)).reshape(
            block_rows, labels_dev, joint_width
        )
        return (
            pred_sum + jnp.sum(tanh_grad, axis=0),
            (joint_cells, logit_grad, jnp.sum(tanh_grad, axis=1)),
        )

    inputs = (
        encoded.reshape(-1, block_rows, joint_width),
        blank_weight.reshape(-1, block_rows, labels_dev),
        label_weight.reshape(-1, block_rows, labels_dev),
    )
    pred_sum, stacked = lax.scan(
        joint_step, jnp.zeros((labels_dev, joint_width), jnp.float32), inputs
    )
    joint_all = stacked[0].reshape(-1, joint_width)
    grad_all = stacked[1].reshape(-1, vocab_size)
    enc_parts = stacked[2].reshape(frames_dev, joint_width)
    enc_grad = lax.psum_scatter(enc_parts, ("labels", "hidden"), scatter_dimension=0, tiled=True)
    pred_grad = lax.psum(pred_sum, "frames")
    n_frames = lax.axis_size("frames")
    n_group = lax.axis_size("labels") * lax.axis_size("hidden")
    total_cells = frames_dev * n_frames * labels_dev * n_group
    head_sum = lax.psum_scatter(
        lax.dot_general(
            grad_all, joint_all, (((0,), (0,)), ((), ())), preferred_element_type=jnp.float32
        ),
        ("frames", "labels", "hidden"),
        scatter_dimension=0,
        tiled=True,
    )
    return (enc_grad, pred_grad, head_sum / math.sqrt(total_cells))


def solution(mesh):
    placed = (
        P("frames", None),
        P(None, "hidden"),
        P("hidden", None),
        P(("labels", "hidden"), None),
        P(),
        P("frames", ("labels", "hidden")),
        P("frames", ("labels", "hidden")),
        P(("labels", "hidden")),
    )
    return jax.shard_map(
        on_device,
        mesh=mesh,
        in_specs=placed,
        out_specs=(
            P(("frames", "labels", "hidden"), None),
            P(("labels", "hidden"), None),
            P(("frames", "labels", "hidden"), None),
        ),
        check_vma=False,
    )
```

profile of v0, /device:TPU:1, one launch (start us, length us, event | category | flops | bytes accessed | tf_op | source)
XLA Modules:
  0.0 650.0 jit_solution(10384635351723706598)
XLA Ops:
  7.3 1.5 copy-done
  8.8 2.8 fusion.8
  12.0 50.4 %all-reduce.6.cloned.1.call-done = f32[4,32,640]{2,1,0:T(8,128)} async-done(((f32[4,32,640]{2,1,0:T(8,128)}), f32[4,32,640]{2,1,0:T(8,128)}) %all-reduce.6.cloned.1.call-update) | async-done | bytes 327696 | tf_op jit(solution)/shard_map/psum | solution.py:20
  62.4 56.8 %while.17 = (s32[]{:T(128)}, f32[16,640]{1,0:T(8,128)S(1)}, bf16[4,512,640]{2,1,0:T(8,128)(2,1)}, bf16[4,512,1024]{2,1,0:T(8,128)(2,1)}, f32[4,32,640]{2,1,0:T(8...) while((s32[]{:T(128)}, f32[16,640]{1,0:T(8,128)S(1)}, ...), condition=%wide.region_6.7_spmd.clone, body=%wide.region_1.6_spmd.clone.sunk | while | flops 1350033408 | bytes 32403152 | solution.py:62
  63.6 2.4 fusion.33
  66.0 1.4 copy-done.1
  68.1 3.4 bitcast_dynamic-update-slice_fusion.6
  71.5 2.1 bitcast_reduce_fusion.2
  74.3 1.4 reduce_sum.37
  77.8 2.4 fusion.33
  80.2 1.4 copy-done.1
  82.3 3.4 bitcast_dynamic-update-slice_fusion.6
  85.7 2.2 bitcast_reduce_fusion.2
  88.5 1.4 reduce_sum.37
  92.0 2.4 fusion.33
  94.4 1.4 copy-done.1
  96.5 3.4 bitcast_dynamic-update-slice_fusion.6
  99.9 2.1 bitcast_reduce_fusion.2
  102.7 1.4 reduce_sum.37
  104.1 0.9 bitcast_dynamic-update-slice_fusion.7
  106.2 2.4 fusion.33
  108.6 1.4 copy-done.1
  110.7 3.4 bitcast_dynamic-update-slice_fusion.6
  114.1 2.2 bitcast_reduce_fusion.2
  116.9 1.4 reduce_sum.37
  118.3 0.9 bitcast_dynamic-update-slice_fusion.7
  119.3 8.0 %convolution_bitcast_fusion = f32[1024,640]{1,0:T(8,128)} fusion(bf16[4,512,1024]{2,1,0:T(8,128)(2,1)} %get-tuple-element.70, bf16[4,512,640]{2,1,0:T(8,128)(2,1)} %get-tuple-element.71), kind=kOutput, calls=%fused_computation.19 | convolution fusion | flops 2684354560 | bytes 9437184 | tf_op jit(solution)/shard_map/dot_general | solution.py:74
  129.3 28.4 %psum.15 = f32[16,640]{1,0:T(8,128)} all-reduce(f32[16,640]{1,0:T(8,128)S(1)} %get-tuple-element.69), channel_id=1, replica_groups=mesh['frames'=8,'labels'=8,'hidden'=4] {'frames'}, use_global_device_ids=true, to_apply=%region_8.9 | all-reduce | flops 10240 | bytes 81920 | tf_op jit(solution)/shard_map/psum | solution.py:69
  157.6 215.6 %all-reduce.8.cloned.1.call-done = f32[128,640]{1,0:T(8,128)} async-done(((f32[128,640]{1,0:T(8,128)}), f32[128,640]{1,0:T(8,128)}) %all-reduce.8.cloned.1.call-update) | async-done | bytes 327696
  373.2 1.3 constant_dynamic-slice_fusion.2
  374.5 267.6 %all-reduce.10.cloned.1.call-done = f32[1024,640]{1,0:T(8,128)} async-done(((f32[1024,640]{1,0:T(8,128)}), f32[1024,640]{1,0:T(8,128)}) %all-reduce.10.cloned.1.call-update) | async-done | bytes 2621456
  642.2 1.3 dynamic-slice_multiply_fusion
  (84 shorter events, 13.6 us)
Async XLA Ops:
  7.2 1.6 copy-start
  7.2 4.5 copy-start.4
  7.2 4.6 copy-start.5
  7.2 4.7 copy-start.3
  7.2 4.7 copy-start.6
  7.2 55.2 %all-reduce.6.cloned.1.call-start = ((), (), s32[]{:S(2)}) async-start(), calls=%async_computation | async-start | bytes 655360 | tf_op jit(solution)/shard_map/psum | solution.py:20
  11.6 361.6 %all-reduce.8.cloned.1.call-start = ((), (), s32[]{:S(2)}) async-start(), calls=%async_computation.1 | async-start | bytes 655360
  66.0 1.4 copy-start.1
  68.1 3.4 copy-start.2
  80.2 1.4 copy-start.1
  82.3 3.5 copy-start.2
  94.4 1.4 copy-start.1
  96.5 3.4 copy-start.2
  108.6 1.4 copy-start.1
  110.7 3.4 copy-start.2
  119.3 522.9 %all-reduce.10.cloned.1.call-start = ((), (), s32[]{:S(2)}) async-start(), calls=%async_computation.2 | async-start | bytes 5242880
  127.3 0.7 copy-start.7
Sparse Core Ops, SparseCore 0:
  11.7 50.6 all-reduce.5
  119.4 253.7 all-reduce.7
  378.7 263.4 all-reduce.9
where the time goes:
time: 652 us; the launch traced here: 650 us
  waiting for transfers between devices  534 us (82%)
  matrix products  29 us (4%)
  blocking collectives  28.4 us (4%)
  other arithmetic  23.8 us (4%)
  local copies, waits for them, and re-layouts  20.3 us (3%)
  between operations  14.5 us (2%)
    unnamed x5, waiting for transfers between devices  483 us
    psum x1, waiting for transfers between devices, on_device(): encoded = lax.psum(partial_enc, 'hidden')  50.4 us
    psum x1, blocking collectives, on_device(): pred_grad = lax.psum(pred_sum, 'frames')  28.4 us
    dynamic_update_slice x4, other arithmetic, on_device(): lax.scan(joint_step, jnp.zeros((labels_dev, joint_width), jnp.float32), i...  13.6 us
  transfers between devices with their start and end apart: 3, of which 3 were waited for; matrix products, arithmetic and copies ran while one was open for 2% of the time, Pallas kernels for 0%

commit v1 on v0

v1 whole, which is shorter than its diff:
```python
import math

import jax
import jax.numpy as jnp
from jax import lax
from jax.experimental import pallas as pl
from jax.experimental.pallas import tpu as pltpu
from jax.sharding import PartitionSpec as P

F32 = jnp.float32
BF16 = jnp.bfloat16
JD = 640
VOCAB = 1024
CH = 4
FT = 8
LB = 64
CELLS = FT * LB
RB = 16
SCALE = 1.0 / math.sqrt(1024 * 512)


def send(src, dst, send_sem, recv_sem, device):
    pltpu.make_async_remote_copy(
        src_ref=src,
        dst_ref=dst,
        send_sem=send_sem,
        recv_sem=recv_sem,
        device_id=device,
        device_id_type=pl.DeviceIdType.MESH,
    ).start()


def drain(ref, sem):
    pltpu.make_async_copy(ref, ref, sem).wait()


def kernel(
    feat_hbm, up_hbm, down_hbm, pred_in, w_hbm, blank_in, label_in, targets,
    enc_out, pred_out, head_out,
    feat, up, down, w, load_sem,
    msg, msg_r, msg_ss, msg_rs,
    part, part_r, part_ss, part_rs,
    pred64, wsum, wblank, wlabel, tgt64,
    joint, lg, grad, jg,
    encp, encp_r, encp_ss, encp_rs,
    predp, predp_r, predp_ss, predp_rs,
    predb, predb_r, predb_ss, predb_rs,
    hab, hc, h1ab, h1c, h1ab_ss, h1ab_rs, h1c_ss, h1c_rs,
    p1a, p1b, p1c, p1_ss, p1_rs,
    a1, b1, c1, p2a, p2b, p2c, p2_ss, p2_rs,
    ab2, c2, p3ab, p3c, p3_ss, p3_rs,
    fin, fin_ss, fin_rs,
):
    f = lax.axis_index("frames")
    z = lax.axis_index("labels")
    h = lax.axis_index("hidden")
    y, x_lo = f // 2, f % 2
    x_hi, core = h // 2, h % 2
    x = x_hi * 2 + x_lo

    loads = []
    for n, (a, b) in enumerate(((feat_hbm, feat), (up_hbm, up), (down_hbm, down), (w_hbm, w))):
        cp = pltpu.make_async_copy(a, b, load_sem.at[n])
        cp.start()
        loads.append(cp)

    def h_peer(k):
        return {"hidden": (h + k) % 4}

    def z_peer(k):
        return {"labels": (z + k) % 8}

    def y_peer(k):
        return {"frames": ((y + k) % 4) * 2 + x_lo}

    def x_peer(k):
        xx = (x + k) % 4
        return {"frames": y * 2 + xx % 2, "hidden": (xx // 2) * 2 + core}

    def f_peer(k):
        return {"frames": (f + k) % 8}

    partner = {"hidden": x_hi * 2 + (1 - core)}

    barrier = pltpu.get_barrier_semaphore()
    greeted = [h_peer(k) for k in (1, 2, 3)] + [z_peer(k) for k in range(1, 8)]
    greeted += [f_peer(k) for k in range(1, 8)] + [x_peer(k) for k in (1, 3)]
    for device in greeted:
        pl.semaphore_signal(barrier, inc=1, device_id=device, device_id_type=pl.DeviceIdType.MESH)

    wcat = jnp.concatenate([blank_in[...], label_in[...]], axis=0)
    row = lax.broadcasted_iota(jnp.int32, (256, 128), 0)
    lane = lax.broadcasted_iota(jnp.int32, (256, 128), 1)
    slot = lane % 32
    tcol = jnp.zeros((16, 128), jnp.int32)
    trow = lax.broadcasted_iota(jnp.int32, (16, 128), 0)
    tlane = lax.broadcasted_iota(jnp.int32, (16, 128), 1)
    for i in range(16):
        tcol = jnp.where(trow == i, targets[i], tcol)
    tfloat = jnp.where(tlane == 64, tcol.astype(F32), 0.0)
    pred_wide = pred_in[...].astype(F32)
    for k in range(4):
        peer = (h + k) % 4
        frame = (slot // 4) * 16 + peer * 4 + slot % 4
        pick = ((row // 128) == (lane // 32)) & ((row % 128) == frame)
        moved = lax.dot_general(
            wcat, pick.astype(F32), (((0,), (0,)), ((), ())),
            preferred_element_type=F32, precision=lax.Precision.HIGHEST,
        )
        msg[k, :, 0:JD] = pred_wide
        msg[k, :, JD:JD + 128] = moved + tfloat

    prow = lax.broadcasted_iota(jnp.int32, (128, 128), 0)
    pcol = lax.broadcasted_iota(jnp.int32, (128, 128), 1)
    pr = prow % 8
    pframe = ((prow // 32) * 2 + pr // 4) * 16 + ((h + (prow // 8) % 4) % 4) * 4 + pr % 4
    perm = (pcol == pframe).astype(F32).astype(BF16)
    loads[0].wait()
    feat_p = jnp.dot(perm, feat[...], preferred_element_type=F32).astype(BF16)

    pl.semaphore_wait(barrier, len(greeted))
    for k in (1, 2, 3):
        send(msg.at[k], msg_r.at[k - 1], msg_ss, msg_rs, h_peer(k))

    loads[1].wait()
    hidden = jnp.maximum(jnp.dot(feat_p, up[...], preferred_element_type=F32), 0.0).astype(BF16)
    loads[2].wait()
    enc = jnp.dot(hidden, down[...], preferred_element_type=F32)
    for c in range(CH):
        for k in range(4):
            r = c * 32 + k * 8
            part[c, k] = enc[r:r + 8, :]
    for c in range(CH):
        for k in (1, 2, 3):
            send(part.at[c, k], part_r.at[c, k - 1], part_ss, part_rs.at[c], h_peer(k))

    drain(msg_r, msg_rs)
    for k in range(4):
        src = msg.at[0] if k == 0 else msg_r.at[k - 1]
        rows = slice(k * 16, k * 16 + 16)
        pred64[rows, :] = src[:, 0:JD]
        tail = src[:, JD:JD + 128]
        tgt64[rows, :] = jnp.broadcast_to(tail[:, 64:65], (16, 128))
        for t in range(CH * FT):
            r = t * LB + k * 16
            b = jnp.broadcast_to(tail[:, t:t + 1], (16, 128))
            l = jnp.broadcast_to(tail[:, 32 + t:33 + t], (16, 128))
            wsum[r:r + 16, :] = b + l
            wblank[r:r + 16, :] = b
            wlabel[r:r + 16, :] = l
    loads[3].wait()

    vocab_id = lax.broadcasted_iota(jnp.int32, (RB, 128), 1).astype(F32)

    def forward(c, carry):
        drain(part_r.at[c], part_rs.at[c])
        enc8 = part[c, 0] + part_r[c, 0] + part_r[c, 1] + part_r[c, 2]
        for t in range(FT):
            cells = jnp.tanh(pred64[...] + enc8[t:t + 1, :])
            joint[pl.ds(pl.multiple_of(c * CELLS + t * LB, LB), LB), :] = cells.astype(BF16)
        base = pl.multiple_of(c * CELLS, CELLS)
        lg[...] = jnp.dot(joint[pl.ds(base, CELLS), :], w[...], preferred_element_type=F32)

        def soft(i, carry):
            at = pl.multiple_of(i * RB, RB)
            rows = pl.ds(at, RB)
            cell = pl.ds(pl.multiple_of(base + i * RB, RB), RB)
            tg = tgt64[pl.ds(pl.multiple_of((i % (LB // RB)) * RB, RB), RB), :]
            tiles = [lg[rows, n * 128:n * 128 + 128] for n in range(8)]
            m = tiles[0]
            for tile in tiles[1:]:
                m = jnp.maximum(m, tile)
            top = jnp.max(m, axis=1, keepdims=True)
            exps = [jnp.exp(tile - top) for tile in tiles]
            s = exps[0]
            for e in exps[1:]:
                s = s + e
            total = jnp.sum(s, axis=1, keepdims=True)
            scale = wsum[cell, :] / total
            lw = wlabel[cell, :]
            for n in range(8):
                g = exps[n] * scale - jnp.where(vocab_id == tg - float(n * 128), lw, 0.0)
                if n == 0:
                    g = g - jnp.where(vocab_id == 0.0, wblank[cell, :], 0.0)
                grad[cell, n * 128:n * 128 + 128] = g.astype(BF16)
            return carry

        lax.fori_loop(0, CELLS // RB, soft, 0, unroll=2)
        return carry

    lax.fori_loop(0, CH, forward, 0)

    def head_block(i):
        yy = (y + 1 + i) % 4
        col = pl.multiple_of(yy * 256, 256)
        block = lax.dot_general(
            grad[:, pl.ds(col, 256)], joint[...], (((0,), (0,)), ((), ())),
            preferred_element_type=F32,
        )
        for t in range(32):
            xl, zz, xh = t // 16, (t // 2) % 8, t % 2
            xx = xh * 2 + xl
            rows = block[t * 8:t * 8 + 8, :]
            hab[0, yy, 0, xx * 8 + zz] = rows[:, 0:128]
            hab[0, yy, 1, xx * 8 + zz] = rows[:, 128:256]
            hc[yy, zz * 4 + xx] = rows[:, 256:384]
            hab[1, yy, 0, xx * 8 + zz] = rows[:, 384:512]
            hab[1, yy, 1, xx * 8 + zz] = rows[:, 512:640]
        send(hab.at[1 - core, yy], h1ab.at[yy], h1ab_ss, h1ab_rs.at[yy], partner)

        @pl.when(core == 1)
        def _():
            send(hc.at[yy], h1c.at[yy], h1c_ss, h1c_rs.at[yy], partner)

    def head_spread(i):
        yy = (y + 1 + i) % 4
        drain(h1ab.at[yy], h1ab_rs.at[yy])
        hab[core, yy] = hab[core, yy] + h1ab[yy]
        for k in (1, 2, 3):
            at = pl.multiple_of(((x + k) % 4) * 8, 8)
            send(hab.at[core, yy, 0, pl.ds(at, 8)], p1a.at[k - 1, yy], p1_ss.at[0], p1_rs.at[0], x_peer(k))

        @pl.when(i < 3)
        def _():
            send(hab.at[core, yy, 1], p1b.at[i], p1_ss.at[1], p1_rs.at[1], {"frames": yy * 2 + x_lo})

        @pl.when(core == 0)
        def _():
            drain(h1c.at[yy], h1c_rs.at[yy])
            hc[yy] = hc[yy] + h1c[yy]
            for k in range(1, 8):
                at = pl.multiple_of(((z + k) % 8) * 4, 4)
                send(hc.at[yy, pl.ds(at, 4)], p1c.at[k - 1, yy], p1_ss.at[2], p1_rs.at[2], z_peer(k))

    def head_step(i, carry):
        head_block(i)

        @pl.when(i > 0)
        def _():
            head_spread(i - 1)

        return carry

    lax.fori_loop(0, 4, head_step, 0)

    predp[...] = jnp.zeros_like(predp)

    def backward(c, carry):
        base = pl.multiple_of(c * CELLS, CELLS)
        jg[...] = lax.dot_general(
            grad[pl.ds(base, CELLS), :], w[...], (((1,), (1,)), ((), ())), preferred_element_type=F32
        )
        for n in range(5):
            cols = slice(n * 128, n * 128 + 128)
            acc = predp[:, cols]
            for t in range(FT):
                cells = joint[pl.ds(pl.multiple_of(base + t * LB, LB), LB), cols].astype(F32)
                tg = jg[t * LB:t * LB + LB, cols] * (1.0 - cells * cells)
                acc = acc + tg
                encp[c * 2 + t // 4, t % 4:t % 4 + 1, cols] = jnp.sum(tg, axis=0, keepdims=True)
            predp[:, cols] = acc
        return carry

    backward(0, 0)
    head_spread(3)
    lax.fori_loop(1, CH, backward, 0)

    for k in range(1, 8):
        send(encp.at[(z + k) % 8], encp_r.at[k - 1], encp_ss, encp_rs, z_peer(k))
    for k in (1, 2, 3):
        send(predp.at[pl.ds(k * 16, 16)], predp_r.at[k - 1], predp_ss, predp_rs, h_peer(4 - k))

    drain(p1a, p1_rs.at[0])
    own = pl.ds(pl.multiple_of(x * 8, 8), 8)
    for yy in range(4):
        a1[yy] = hab[core, yy, 0, own] + p1a[0, yy] + p1a[1, yy] + p1a[2, yy]
    for k in (1, 2, 3):
        send(a1.at[(y + k) % 4], p2a.at[k - 1], p2_ss.at[0], p2_rs.at[0], y_peer(k))
    drain(p1b, p1_rs.at[1])
    b1[...] = hab[core, y, 1] + p1b[0] + p1b[1] + p1b[2]
    for k in (1, 2, 3):
        at = pl.multiple_of(((x + k) % 4) * 8, 8)
        send(b1.at[pl.ds(at, 8)], p2b.at[k - 1], p2_ss.at[1], p2_rs.at[1], x_peer(k))

    @pl.when(core == 0)
    def _():
        drain(p1c, p1_rs.at[2])
        mine = pl.ds(pl.multiple_of(z * 4, 4), 4)
        for yy in range(4):
            tot = hc[yy, mine]
            for k in range(7):
                tot = tot + p1c[k, yy]
            c1[yy] = tot
        for k in (1, 2, 3):
            send(c1.at[(y + k) % 4], p2c.at[k - 1], p2_ss.at[2], p2_rs.at[2], y_peer(k))

    drain(predp_r, predp_rs)
    predb[...] = predp[0:16, :] + predp_r[0] + predp_r[1] + predp_r[2]
    for k in range(1, 8):
        send(predb, predb_r.at[k - 1], predb_ss, predb_rs, f_peer(k))

    drain(p2a, p2_rs.at[0])
    a2 = a1[y] + p2a[0] + p2a[1] + p2a[2]
    drain(p2b, p2_rs.at[1])
    b2 = b1[own] + p2b[0] + p2b[1] + p2b[2]
    for zz in range(8):
        ab2[zz, 0] = a2[zz]
        ab2[zz, 1] = b2[zz]
    for k in range(1, 8):
        send(ab2.at[(z + k) % 8], p3ab.at[k - 1], p3_ss.at[0], p3_rs.at[0], z_peer(k))

    @pl.when(core == 0)
    def _():
        drain(p2c, p2_rs.at[2])
        c2[...] = c1[y] + p2c[0] + p2c[1] + p2c[2]
        for k in (1, 2, 3):
            send(c2.at[(x + k) % 4], p3c.at[k - 1], p3_ss.at[1], p3_rs.at[1], x_peer(k))

    drain(encp_r, encp_rs)
    tot = encp[z]
    for k in range(7):
        tot = tot + encp_r[k]
    enc_out[...] = tot

    drain(predb_r, predb_rs)
    tot = predb[...]
    for k in range(7):
        tot = tot + predb_r[k]
    pred_out[...] = tot

    drain(p3ab, p3_rs.at[0])
    tot = ab2[z]
    for k in range(7):
        tot = tot + p3ab[k]
    fin[core, 0:2] = tot

    @pl.when(core == 0)
    def _():
        drain(p3c, p3_rs.at[1])
        fin[0, 2] = c2[x] + p3c[0] + p3c[1] + p3c[2]
        send(fin.at[0], fin.at[0], fin_ss, fin_rs, partner)
        drain(fin.at[1, pl.ds(0, 2)], fin_rs)
        drain(fin.at[0], fin_ss)

    @pl.when(core == 1)
    def _():
        send(fin.at[1, pl.ds(0, 2)], fin.at[1, pl.ds(0, 2)], fin_ss, fin_rs, partner)
        drain(fin.at[0], fin_rs)
        drain(fin.at[1, pl.ds(0, 2)], fin_ss)

    for n in range(5):
        tile = fin[n // 3, n % 3]
        mine = jnp.where(core == 0, tile[0:4, :], tile[4:8, :])
        head_out[:, n * 128:n * 128 + 128] = mine * SCALE

    drain(msg_r, msg_ss)
    drain(part_r, part_ss)
    drain(encp_r, encp_ss)
    drain(predp_r, predp_ss)
    drain(predb_r, predb_ss)
    drain(h1ab, h1ab_ss)
    drain(p1a, p1_ss.at[0])
    drain(p1b, p1_ss.at[1])
    drain(p2a, p2_ss.at[0])
    drain(p2b, p2_ss.at[1])
    drain(p3ab, p3_ss.at[0])

    @pl.when(core == 0)
    def _():
        drain(p1c, p1_ss.at[2])
        drain(p2c, p2_ss.at[2])
        drain(p3c, p3_ss.at[1])

    @pl.when(core == 1)
    def _():
        drain(h1c, h1c_ss)


def on_device(features, up_weight, down_weight, predictor, out_weight, blank_weight, label_weight, targets):
    V = pltpu.VMEM
    dma = pltpu.SemaphoreType.DMA
    scratch = [
        V((128, 1024), BF16), V((1024, 1024), BF16), V((1024, JD), BF16), V((JD, VOCAB), BF16), dma((4,)),
        V((4, 16, JD + 128), F32), V((3, 16, JD + 128), F32), dma, dma,
        V((CH, 4, 8, JD), F32), V((CH, 3, 8, JD), F32), dma, dma((CH,)),
        V((LB, JD), F32), V((2048, 128), F32), V((2048, 128), F32), V((2048, 128), F32), V((LB, 128), F32),
        V((2048, JD), BF16), V((CELLS, VOCAB), F32), V((2048, VOCAB), BF16), V((CELLS, JD), F32),
        V((8, 4, JD), F32), V((7, 4, JD), F32), dma, dma,
        V((LB, JD), F32), V((3, 16, JD), F32), dma, dma,
        V((16, JD), F32), V((7, 16, JD), F32), dma, dma,
        V((2, 4, 2, 32, 8, 128), F32), V((4, 32, 8, 128), F32),
        V((4, 2, 32, 8, 128), F32), V((4, 32, 8, 128), F32), dma, dma((4,)), dma, dma((4,)),
        V((3, 4, 8, 8, 128), F32), V((3, 32, 8, 128), F32), V((7, 4, 4, 8, 128), F32), dma((3,)), dma((3,)),
        V((4, 8, 8, 128), F32), V((32, 8, 128), F32), V((4, 4, 8, 128), F32),
        V((3, 8, 8, 128), F32), V((3, 8, 8, 128), F32), V((3, 4, 8, 128), F32), dma((3,)), dma((3,)),
        V((8, 2, 8, 128), F32), V((4, 8, 128), F32), V((7, 2, 8, 128), F32), V((3, 8, 128), F32),
        dma((2,)), dma((2,)),
        V((2, 3, 8, 128), F32), dma, dma,
    ]
    hbm = pl.BlockSpec(memory_space=pl.ANY)
    vmem = pl.BlockSpec(memory_space=pltpu.VMEM)
    smem = pl.BlockSpec(memory_space=pltpu.SMEM)
    return pl.pallas_call(
        kernel,
        out_shape=(
            jax.ShapeDtypeStruct((4, JD), F32),
            jax.ShapeDtypeStruct((16, JD), F32),
            jax.ShapeDtypeStruct((4, JD), F32),
        ),
        in_specs=[hbm, hbm, hbm, vmem, hbm, vmem, vmem, smem],
        out_specs=(vmem, vmem, vmem),
        scratch_shapes=scratch,
        compiler_params=pltpu.CompilerParams(
            collective_id=0, has_side_effects=True, vmem_limit_bytes=60 * 1024 * 1024
        ),
    )(features, up_weight, down_weight, predictor, out_weight, blank_weight, label_weight, targets)


def solution(mesh):
    placed = (
        P("frames", None),
        P(None, "hidden"),
        P("hidden", None),
        P(("labels", "hidden"), None),
        P(),
        P("frames", ("labels", "hidden")),
        P("frames", ("labels", "hidden")),
        P(("labels", "hidden")),
    )
    return jax.shard_map(
        on_device,
        mesh=mesh,
        in_specs=placed,
        out_specs=(
            P(("frames", "labels", "hidden"), None),
            P(("labels", "hidden"), None),
            P(("frames", "labels", "hidden"), None),
        ),
        check_vma=False,
    )
```

time: 652 us -> 64.9 us (0.10)
  waiting for transfers between devices: 534 us -> 0 us
  Pallas kernels: 0 us -> 57 us
  matrix products: 29 us -> 0 us
  blocking collectives: 28.4 us -> 0 us
  other arithmetic: 23.8 us -> 0 us
  between operations: 14.5 us -> 0.64 us
  local copies, waits for them, and re-layouts: 20.3 us -> 6.83 us
    unnamed x5 -> x0, waiting for transfers between devices: 483 us -> none
    pallas_call x0 -> x1, Pallas kernels: none -> 57 us  [on_device(): pl.pallas_call(kernel, out_shape=(jax.ShapeDtypeStruct((4, JD), F32), jax...]
    psum x1 -> x0, waiting for transfers between devices: 50.4 us -> none  [on_device(): encoded = lax.psum(partial_enc, 'hidden')]
    dot_general x10 -> x0, matrix products: 29 us -> none  [the longest x4 9.54 us: joint_step(): jnp.dot(joint_cells, out_weight, preferred_element_type=jnp.float32)]
    psum x1 -> x0, blocking collectives: 28.4 us -> none  [on_device(): pred_grad = lax.psum(pred_sum, 'frames')]
    dynamic_update_slice x4 -> x0, other arithmetic: 13.6 us -> none  [on_device(): lax.scan(joint_step, jnp.zeros((labels_dev, joint_width), jnp.float32), i...]
    reduce_sum x8 -> x0, other arithmetic: 7.62 us -> none  [the longest x4 5.57 us: joint_step(): jnp.sum(tanh_grad, axis=0)]
  transfers between devices with their start and end apart: 3 -> 0, of which waited for: 3 -> 0; matrix products, arithmetic and copies ran while one was open for 2% -> 0% of each run, Pallas kernels for 0% -> 0%
where the time goes in v1:
time: 64.9 us; the launch traced here: 64.5 us
  Pallas kernels  57 us (88%)
  local copies, waits for them, and re-layouts  6.83 us (11%)
    pallas_call x1, Pallas kernels, on_device(): pl.pallas_call(kernel, out_shape=(jax.ShapeDtypeStruct((4, JD), F32), jax...  57 us
    unnamed x5, local copies, waits for them, and re-layouts  6.83 us

profile of v1, /device:TPU:1, one launch (start us, length us, event | category | flops | bytes accessed | tf_op | source)
XLA Modules:
  0.0 64.5 jit_solution(6674859435194929596)
XLA Ops:
  0.6 1.4 %copy.11.blank_in = f32[128,16]{1,0:T(8,128)} copy(f32[128,16]{0,1:T(8,128)} %param.13) | data formatting | bytes 16384 | tf_op args[5]
  2.0 1.4 %copy.12.label_in = f32[128,16]{1,0:T(8,128)} copy(f32[128,16]{0,1:T(8,128)} %param.14) | data formatting | bytes 16384 | tf_op args[6]
  3.5 57.0 %shard_map.103 = (f32[4,640]{1,0:T(4,128)}, f32[16,640]{1,0:T(8,128)}, f32[4,640]{1,0:T(4,128)}) custom-call(bf16[128,1024]{1,0:T(8,128)(2,1)} %feat_hbm.1, bf16[1024,1024]{1,0:T(8,128)(2,1)} %up_hbm.1, bf16[1024,640]{1,0:T(8,128)(2,1)} %down_hbm.1, bf16[16,640]{1,0:T(8,128)(2,1)} %pred_in.1, bf16[640,1024]{1,0:T(8,128)(2,1)} %w_hbm.1, ...), custom_call_target="tpu_custom_call" | custom-call | tf_op jit(solution)/shard_map/pallas_call | solution.py:403
  60.5 1.3 %copy.16 = f32[4,640]{1,0:T(4,128)} copy(f32[4,640]{1,0:T(4,128)} %get-tuple-element.6) | data formatting | bytes 20480
  61.8 1.4 %copy.17 = f32[16,640]{1,0:T(8,128)} copy(f32[16,640]{1,0:T(8,128)} %get-tuple-element.7) | data formatting | bytes 81920
  63.2 1.3 %copy.18 = f32[4,640]{1,0:T(4,128)} copy(f32[4,640]{1,0:T(4,128)} %get-tuple-element.8) | data formatting | bytes 20480

commit v2 on v1

--- a/solution.py
+++ b/solution.py
@@ -35,12 +35,12 @@
 
 
 def kernel(
-    feat_hbm, up_hbm, down_hbm, pred_in, w_hbm, blank_in, label_in, targets,
+    feat_hbm, up_hbm, down_hbm, pred_hbm, w_hbm, blank_hbm, label_hbm, targets,
     enc_out, pred_out, head_out,
-    feat, up, down, w, load_sem,
+    feat, up, down, w, pred_in, blank_in, label_in, load_sem,
     msg, msg_r, msg_ss, msg_rs,
     part, part_r, part_ss, part_rs,
-    pred64, wsum, wblank, wlabel, tgt64,
+    pred64, wsum, wblank, wlabel, hot,
     joint, lg, grad, jg,
     encp, encp_r, encp_ss, encp_rs,
     predp, predp_r, predp_ss, predp_rs,
@@ -48,8 +48,8 @@
     hab, hc, h1ab, h1c, h1ab_ss, h1ab_rs, h1c_ss, h1c_rs,
     p1a, p1b, p1c, p1_ss, p1_rs,
     a1, b1, c1, p2a, p2b, p2c, p2_ss, p2_rs,
-    ab2, c2, p3ab, p3c, p3_ss, p3_rs,
-    fin, fin_ss, fin_rs,
+    ab2, c2, p3own, p3oth, p3c, p3d, p3_ss, p3_rs,
+    fin,
 ):
     f = lax.axis_index("frames")
     z = lax.axis_index("labels")
@@ -58,12 +58,6 @@
     x_hi, core = h // 2, h % 2
     x = x_hi * 2 + x_lo
 
-    loads = []
-    for n, (a, b) in enumerate(((feat_hbm, feat), (up_hbm, up), (down_hbm, down), (w_hbm, w))):
-        cp = pltpu.make_async_copy(a, b, load_sem.at[n])
-        cp.start()
-        loads.append(cp)
-
     def h_peer(k):
         return {"hidden": (h + k) % 4}
 
@@ -80,51 +74,61 @@
     def f_peer(k):
         return {"frames": (f + k) % 8}
 
-    partner = {"hidden": x_hi * 2 + (1 - core)}
+    other = x_hi * 2 + (1 - core)
+    partner = {"hidden": other}
+
+    def z_other(k):
+        return {"labels": (z + k) % 8, "hidden": other}
+
+    def x_other(k):
+        xx = (x + k) % 4
+        return {"frames": y * 2 + xx % 2, "hidden": (xx // 2) * 2 + (1 - core)}
 
     barrier = pltpu.get_barrier_semaphore()
     greeted = [h_peer(k) for k in (1, 2, 3)] + [z_peer(k) for k in range(1, 8)]
     greeted += [f_peer(k) for k in range(1, 8)] + [x_peer(k) for k in (1, 3)]
+    greeted += [z_other(k) for k in range(1, 8)] + [x_other(k) for k in (1, 3)]
     for device in greeted:
         pl.semaphore_signal(barrier, inc=1, device_id=device, device_id_type=pl.DeviceIdType.MESH)
 
-    wcat = jnp.concatenate([blank_in[...], label_in[...]], axis=0)
-    row = lax.broadcasted_iota(jnp.int32, (256, 128), 0)
-    lane = lax.broadcasted_iota(jnp.int32, (256, 128), 1)
-    slot = lane % 32
-    tcol = jnp.zeros((16, 128), jnp.int32)
-    trow = lax.broadcasted_iota(jnp.int32, (16, 128), 0)
-    tlane = lax.broadcasted_iota(jnp.int32, (16, 128), 1)
-    for i in range(16):
-        tcol = jnp.where(trow == i, targets[i], tcol)
-    tfloat = jnp.where(tlane == 64, tcol.astype(F32), 0.0)
-    pred_wide = pred_in[...].astype(F32)
-    for k in range(4):
-        peer = (h + k) % 4
-        frame = (slot // 4) * 16 + peer * 4 + slot % 4
-        pick = ((row // 128) == (lane // 32)) & ((row % 128) == frame)
-        moved = lax.dot_general(
-            wcat, pick.astype(F32), (((0,), (0,)), ((), ())),
-            preferred_element_type=F32, precision=lax.Precision.HIGHEST,
-        )
-        msg[k, :, 0:JD] = pred_wide
-        msg[k, :, JD:JD + 128] = moved + tfloat
+    pairs = (
+        (feat_hbm, feat), (blank_hbm, blank_in), (label_hbm, label_in), (pred_hbm, pred_in),
+        (up_hbm, up), (down_hbm, down), (w_hbm, w),
+    )
+    loads = [pltpu.make_async_copy(a, b, load_sem.at[n]) for n, (a, b) in enumerate(pairs)]
+    for load in loads:
+        load.start()
 
     prow = lax.broadcasted_iota(jnp.int32, (128, 128), 0)
     pcol = lax.broadcasted_iota(jnp.int32, (128, 128), 1)
     pr = prow % 8
     pframe = ((prow // 32) * 2 + pr // 4) * 16 + ((h + (prow // 8) % 4) % 4) * 4 + pr % 4
     perm = (pcol == pframe).astype(F32).astype(BF16)
-    loads[0].wait()
+    tcol = jnp.zeros((16, 128), jnp.int32)
+    trow = lax.broadcasted_iota(jnp.int32, (16, 128), 0)
+    for i in range(16):
+        tcol = jnp.where(trow == i, targets[i], tcol)
+    tfloat = tcol.astype(F32)
+    lane = lax.broadcasted_iota(jnp.int32, (16, 128), 1) % 16
+    for n in range(4):
+        loads[n].wait()
     feat_p = jnp.dot(perm, feat[...], preferred_element_type=F32).astype(BF16)
+
+    pred_wide = pred_in[...].astype(F32)
+    for d in range(4):
+        msg[d, :, 0:JD] = pred_wide
+        b = pltpu.roll(blank_in[...], (128 - 4 * d) % 128, 1)
+        l = pltpu.roll(label_in[...], (132 - 4 * d) % 128, 1)
+        msg[d, :, JD:JD + 128] = jnp.where(lane < 4, b, jnp.where(lane < 8, l, tfloat))
+
+    loads[4].wait()
+    hidden = jnp.maximum(jnp.dot(feat_p, up[...], preferred_element_type=F32), 0.0).astype(BF16)
 
     pl.semaphore_wait(barrier, len(greeted))
     for k in (1, 2, 3):
-        send(msg.at[k], msg_r.at[k - 1], msg_ss, msg_rs, h_peer(k))
-
-    loads[1].wait()
-    hidden = jnp.maximum(jnp.dot(feat_p, up[...], preferred_element_type=F32), 0.0).astype(BF16)
-    loads[2].wait()
+        send(msg.at[(h + k) % 4], msg_r.at[k - 1], msg_ss, msg_rs, h_peer(k))
+
+    loads[5].wait()
     enc = jnp.dot(hidden, down[...], preferred_element_type=F32)
     for c in range(CH):
         for k in range(4):
@@ -134,39 +138,40 @@
         for k in (1, 2, 3):
             send(part.at[c, k], part_r.at[c, k - 1], part_ss, part_rs.at[c], h_peer(k))
 
+    vocab_id = lax.broadcasted_iota(jnp.int32, (RB, 128), 1).astype(F32)
     drain(msg_r, msg_rs)
     for k in range(4):
-        src = msg.at[0] if k == 0 else msg_r.at[k - 1]
+        src = msg.at[h] if k == 0 else msg_r.at[k - 1]
         rows = slice(k * 16, k * 16 + 16)
         pred64[rows, :] = src[:, 0:JD]
         tail = src[:, JD:JD + 128]
-        tgt64[rows, :] = jnp.broadcast_to(tail[:, 64:65], (16, 128))
+        tg = jnp.broadcast_to(tail[:, 8:9], (16, 128))
+        for n in range(8):
+            hot[rows, n * 128:n * 128 + 128] = jnp.where(vocab_id == tg - float(n * 128), 1.0, 0.0)
         for t in range(CH * FT):
             r = t * LB + k * 16
-            b = jnp.broadcast_to(tail[:, t:t + 1], (16, 128))
-            l = jnp.broadcast_to(tail[:, 32 + t:33 + t], (16, 128))
+            at = (t // 4) * 16 + t % 4
+            b = jnp.broadcast_to(tail[:, at:at + 1], (16, 128))
+            l = jnp.broadcast_to(tail[:, at + 4:at + 5], (16, 128))
             wsum[r:r + 16, :] = b + l
             wblank[r:r + 16, :] = b
             wlabel[r:r + 16, :] = l
-    loads[3].wait()
-
-    vocab_id = lax.broadcasted_iota(jnp.int32, (RB, 128), 1).astype(F32)
-
-    def forward(c, carry):
+    loads[6].wait()
+
+    def logits_of(c):
         drain(part_r.at[c], part_rs.at[c])
         enc8 = part[c, 0] + part_r[c, 0] + part_r[c, 1] + part_r[c, 2]
         for t in range(FT):
             cells = jnp.tanh(pred64[...] + enc8[t:t + 1, :])
-            joint[pl.ds(pl.multiple_of(c * CELLS + t * LB, LB), LB), :] = cells.astype(BF16)
-        base = pl.multiple_of(c * CELLS, CELLS)
-        lg[...] = jnp.dot(joint[pl.ds(base, CELLS), :], w[...], preferred_element_type=F32)
-
-        def soft(i, carry):
-            at = pl.multiple_of(i * RB, RB)
-            rows = pl.ds(at, RB)
-            cell = pl.ds(pl.multiple_of(base + i * RB, RB), RB)
-            tg = tgt64[pl.ds(pl.multiple_of((i % (LB // RB)) * RB, RB), RB), :]
-            tiles = [lg[rows, n * 128:n * 128 + 128] for n in range(8)]
+            joint[c * CELLS + t * LB:c * CELLS + t * LB + LB, :] = cells.astype(BF16)
+        lg[c % 2] = jnp.dot(joint[c * CELLS:c * CELLS + CELLS, :], w[...], preferred_element_type=F32)
+
+    def softmax_of(c):
+        for i in range(CELLS // RB):
+            rows = slice(i * RB, i * RB + RB)
+            cell = slice(c * CELLS + i * RB, c * CELLS + i * RB + RB)
+            label = slice((i * RB) % LB, (i * RB) % LB + RB)
+            tiles = [lg[c % 2, rows, n * 128:n * 128 + 128] for n in range(8)]
             m = tiles[0]
             for tile in tiles[1:]:
                 m = jnp.maximum(m, tile)
@@ -175,20 +180,19 @@
             s = exps[0]
             for e in exps[1:]:
                 s = s + e
-            total = jnp.sum(s, axis=1, keepdims=True)
-            scale = wsum[cell, :] / total
+            scale = wsum[cell, :] / jnp.sum(s, axis=1, keepdims=True)
             lw = wlabel[cell, :]
             for n in range(8):
-                g = exps[n] * scale - jnp.where(vocab_id == tg - float(n * 128), lw, 0.0)
+                g = exps[n] * scale - lw * hot[label, n * 128:n * 128 + 128]
                 if n == 0:
                     g = g - jnp.where(vocab_id == 0.0, wblank[cell, :], 0.0)
                 grad[cell, n * 128:n * 128 + 128] = g.astype(BF16)
-            return carry
-
-        lax.fori_loop(0, CELLS // RB, soft, 0, unroll=2)
-        return carry
-
-    lax.fori_loop(0, CH, forward, 0)
+
+    logits_of(0)
+    for c in range(1, CH):
+        logits_of(c)
+        softmax_of(c - 1)
+    softmax_of(CH - 1)
 
     def head_block(i):
         yy = (y + 1 + i) % 4
@@ -306,15 +310,19 @@
     for zz in range(8):
         ab2[zz, 0] = a2[zz]
         ab2[zz, 1] = b2[zz]
-    for k in range(1, 8):
-        send(ab2.at[(z + k) % 8], p3ab.at[k - 1], p3_ss.at[0], p3_rs.at[0], z_peer(k))
+    for k in range(8):
+        send(ab2.at[(z + k) % 8], p3oth.at[k], p3_ss.at[1], p3_rs.at[1], z_other(k))
+        if k:
+            send(ab2.at[(z + k) % 8], p3own.at[k - 1], p3_ss.at[0], p3_rs.at[0], z_peer(k))
 
     @pl.when(core == 0)
     def _():
         drain(p2c, p2_rs.at[2])
         c2[...] = c1[y] + p2c[0] + p2c[1] + p2c[2]
-        for k in (1, 2, 3):
-            send(c2.at[(x + k) % 4], p3c.at[k - 1], p3_ss.at[1], p3_rs.at[1], x_peer(k))
+        for k in range(4):
+            send(c2.at[(x + k) % 4], p3d.at[k], p3_ss.at[3], p3_rs.at[3], x_other(k))
+            if k:
+                send(c2.at[(x + k) % 4], p3c.at[k - 1], p3_ss.at[2], p3_rs.at[2], x_peer(k))
 
     drain(encp_r, encp_rs)
     tot = encp[z]
@@ -328,30 +336,31 @@
         tot = tot + predb_r[k]
     pred_out[...] = tot
 
-    drain(p3ab, p3_rs.at[0])
+    drain(p3own, p3_rs.at[0])
     tot = ab2[z]
     for k in range(7):
-        tot = tot + p3ab[k]
+        tot = tot + p3own[k]
     fin[core, 0:2] = tot
+    drain(p3oth, p3_rs.at[1])
+    tot = p3oth[0]
+    for k in range(1, 8):
+        tot = tot + p3oth[k]
+    fin[1 - core, 0:2] = tot
 
     @pl.when(core == 0)
     def _():
-        drain(p3c, p3_rs.at[1])
+        drain(p3c, p3_rs.at[2])
         fin[0, 2] = c2[x] + p3c[0] + p3c[1] + p3c[2]
-        send(fin.at[0], fin.at[0], fin_ss, fin_rs, partner)
-        drain(fin.at[1, pl.ds(0, 2)], fin_rs)
-        drain(fin.at[0], fin_ss)
 
     @pl.when(core == 1)
     def _():
-        send(fin.at[1, pl.ds(0, 2)], fin.at[1, pl.ds(0, 2)], fin_ss, fin_rs, partner)
-        drain(fin.at[0], fin_rs)
-        drain(fin.at[1, pl.ds(0, 2)], fin_ss)
+        drain(p3d, p3_rs.at[3])
+        fin[0, 2] = p3d[0] + p3d[1] + p3d[2] + p3d[3]
 
     for n in range(5):
         tile = fin[n // 3, n % 3]
         mine = jnp.where(core == 0, tile[0:4, :], tile[4:8, :])
-        head_out[:, n * 128:n * 128 + 128] = mine * SCALE
+        head_out[:, n * 128:n * 128 + 128] = mine
 
     drain(msg_r, msg_ss)
     drain(part_r, part_ss)
@@ -363,28 +372,37 @@
     drain(p1b, p1_ss.at[1])
     drain(p2a, p2_ss.at[0])
     drain(p2b, p2_ss.at[1])
-    drain(p3ab, p3_ss.at[0])
+    drain(p3own, p3_ss.at[0])
+    drain(p3oth, p3_ss.at[1])
 
     @pl.when(core == 0)
     def _():
         drain(p1c, p1_ss.at[2])
         drain(p2c, p2_ss.at[2])
-        drain(p3c, p3_ss.at[1])
+        drain(p3c, p3_ss.at[2])
+        drain(p3d, p3_ss.at[3])
 
     @pl.when(core == 1)
     def _():
         drain(h1c, h1c_ss)
+
+
+def hand_on(enc_in, pred_in, head_in, enc_out, pred_out, head_out):
+    enc_out[...] = enc_in[...]
+    pred_out[...] = pred_in[...]
+    head_out[...] = head_in[...] * SCALE
 
 
 def on_device(features, up_weight, down_weight, predictor, out_weight, blank_weight, label_weight, targets):
     V = pltpu.VMEM
     dma = pltpu.SemaphoreType.DMA
     scratch = [
-        V((128, 1024), BF16), V((1024, 1024), BF16), V((1024, JD), BF16), V((JD, VOCAB), BF16), dma((4,)),
+        V((128, 1024), BF16), V((1024, 1024), BF16), V((1024, JD), BF16), V((JD, VOCAB), BF16),
+        V((16, JD), BF16), V((16, 128), F32), V((16, 128), F32), dma((7,)),
         V((4, 16, JD + 128), F32), V((3, 16, JD + 128), F32), dma, dma,
         V((CH, 4, 8, JD), F32), V((CH, 3, 8, JD), F32), dma, dma((CH,)),
-        V((LB, JD), F32), V((2048, 128), F32), V((2048, 128), F32), V((2048, 128), F32), V((LB, 128), F32),
-        V((2048, JD), BF16), V((CELLS, VOCAB), F32), V((2048, VOCAB), BF16), V((CELLS, JD), F32),
+        V((LB, JD), F32), V((2048, 128), F32), V((2048, 128), F32), V((2048, 128), F32), V((LB, VOCAB), F32),
+        V((2048, JD), BF16), V((2, CELLS, VOCAB), F32), V((2048, VOCAB), BF16), V((CELLS, JD), F32),
         V((8, 4, JD), F32), V((7, 4, JD), F32), dma, dma,
         V((LB, JD), F32), V((3, 16, JD), F32), dma, dma,
         V((16, JD), F32), V((7, 16, JD), F32), dma, dma,
@@ -393,27 +411,31 @@
         V((3, 4, 8, 8, 128), F32), V((3, 32, 8, 128), F32), V((7, 4, 4, 8, 128), F32), dma((3,)), dma((3,)),
         V((4, 8, 8, 128), F32), V((32, 8, 128), F32), V((4, 4, 8, 128), F32),
         V((3, 8, 8, 128), F32), V((3, 8, 8, 128), F32), V((3, 4, 8, 128), F32), dma((3,)), dma((3,)),
-        V((8, 2, 8, 128), F32), V((4, 8, 128), F32), V((7, 2, 8, 128), F32), V((3, 8, 128), F32),
-        dma((2,)), dma((2,)),
-        V((2, 3, 8, 128), F32), dma, dma,
+        V((8, 2, 8, 128), F32), V((4, 8, 128), F32), V((7, 2, 8, 128), F32), V((8, 2, 8, 128), F32),
+        V((3, 8, 128), F32), V((4, 8, 128), F32), dma((4,)), dma((4,)),
+        V((2, 3, 8, 128), F32),
     ]
     hbm = pl.BlockSpec(memory_space=pl.ANY)
     vmem = pl.BlockSpec(memory_space=pltpu.VMEM)
     smem = pl.BlockSpec(memory_space=pltpu.SMEM)
-    return pl.pallas_call(
+    shapes = (
+        jax.ShapeDtypeStruct((4, JD), F32),
+        jax.ShapeDtypeStruct((16, JD), F32),
+        jax.ShapeDtypeStruct((4, JD), F32),
+    )
+    results = pl.pallas_call(
         kernel,
-        out_shape=(
-            jax.ShapeDtypeStruct((4, JD), F32),
-            jax.ShapeDtypeStruct((16, JD), F32),
-            jax.ShapeDtypeStruct((4, JD), F32),
-        ),
-        in_specs=[hbm, hbm, hbm, vmem, hbm, vmem, vmem, smem],
+        out_shape=shapes,
+        in_specs=[hbm] * 7 + [smem],
         out_specs=(vmem, vmem, vmem),
         scratch_shapes=scratch,
         compiler_params=pltpu.CompilerParams(
             collective_id=0, has_side_effects=True, vmem_limit_bytes=60 * 1024 * 1024
         ),
-    )(features, up_weight, down_weight, predictor, out_weight, blank_weight, label_weight, targets)
+    )(features, up_weight, down_weight, predictor, out_weight, blank_weight.T, label_weight.T, targets)
+    return pl.pallas_call(
+        hand_on, out_shape=shapes, in_specs=[vmem] * 3, out_specs=(vmem,) * 3
+    )(*results)
 
 
 def solution(mesh):

time: 64.9 us -> 46.5 us (0.72)
  Pallas kernels: 57 us -> 45.8 us
  local copies, waits for them, and re-layouts: 6.83 us -> 0 us
    pallas_call x1 -> x2, Pallas kernels: 57 us -> 45.8 us  [the longest x1 44.4 us: on_device(): pl.pallas_call(kernel, out_shape=shapes, in_specs=[hbm] * 7 + [smem], out...]
    unnamed x5 -> x0, local copies, waits for them, and re-layouts: 6.83 us -> none
where the time goes in v2:
time: 46.5 us; the launch traced here: 46.4 us
  Pallas kernels  45.8 us (98%)
  between operations  0.64 us (1%)
    pallas_call x1, Pallas kernels, on_device(): pl.pallas_call(kernel, out_shape=shapes, in_specs=[hbm] * 7 + [smem], out...  44.4 us
    pallas_call x1, Pallas kernels, on_device(): pl.pallas_call(hand_on, out_shape=shapes, in_specs=[vmem] * 3, out_specs=...  1.4 us

profile of v2, /device:TPU:1, one launch (start us, length us, event | category | flops | bytes accessed | tf_op | source)
XLA Modules:
  0.0 46.4 jit_solution(9133840779252675934)
XLA Ops:
  0.6 44.4 %shard_map.103 = (f32[4,640]{1,0:T(4,128)}, f32[16,640]{1,0:T(8,128)}, f32[4,640]{1,0:T(4,128)}) custom-call(bf16[128,1024]{1,0:T(8,128)(2,1)} %feat_hbm.1, bf16[1024,1024]{1,0:T(8,128)(2,1)} %up_hbm.1, bf16[1024,640]{1,0:T(8,128)(2,1)} %down_hbm.1, bf16[16,640]{1,0:T(8,128)(2,1)} %pred_hbm.1, bf16[640,1024]{1,0:T(8,128)(2,1)} %w_hbm.1, f32[16,128]{1,0:T(8,128)} %bitcast.2, ...), custom_call_target="tpu_custom_call" | custom-call | tf_op jit(solution)/shard_map/pallas_call | solution.py:426
  45.0 1.4 %shard_map.104 = (f32[4,640]{1,0:T(4,128)}, f32[16,640]{1,0:T(8,128)}, f32[4,640]{1,0:T(4,128)}) custom-call(f32[4,640]{1,0:T(4,128)} %get-tuple-element.6.enc_in, f32[16,640]{1,0:T(8,128)} %get-tuple-element.7.pred_in, f32[4,640]{1,0:T(4,128)} %get-tuple-element.8.head_in), custom_call_target="tpu_custom_call" | custom-call | tf_op jit(solution)/shard_map/pallas_call | solution.py:436

commit v3 on v2

--- a/solution.py
+++ b/solution.py
@@ -11,9 +11,10 @@
 BF16 = jnp.bfloat16
 JD = 640
 VOCAB = 1024
+FR = 32
+LB = 64
 CH = 4
-FT = 8
-LB = 64
+FT = FR // CH
 CELLS = FT * LB
 RB = 16
 SCALE = 1.0 / math.sqrt(1024 * 512)
@@ -40,13 +41,13 @@
     feat, up, down, w, pred_in, blank_in, label_in, load_sem,
     msg, msg_r, msg_ss, msg_rs,
     part, part_r, part_ss, part_rs,
-    pred64, wsum, wblank, wlabel, hot,
+    pred64, wsum, wblank, wlabel, hot, encacc,
     joint, lg, grad, jg,
     encp, encp_r, encp_ss, encp_rs,
     predp, predp_r, predp_ss, predp_rs,
     predb, predb_r, predb_ss, predb_rs,
     hab, hc, h1ab, h1c, h1ab_ss, h1ab_rs, h1c_ss, h1c_rs,
-    p1a, p1b, p1c, p1_ss, p1_rs,
+    p1a, p1b, p1c, p1_ss, p1a_rs, p1b_rs, p1c_rs,
     a1, b1, c1, p2a, p2b, p2c, p2_ss, p2_rs,
     ab2, c2, p3own, p3oth, p3c, p3d, p3_ss, p3_rs,
     fin,
@@ -58,8 +59,11 @@
     x_hi, core = h // 2, h % 2
     x = x_hi * 2 + x_lo
 
-    def h_peer(k):
-        return {"hidden": (h + k) % 4}
+    def h_of(s):
+        return ((x_hi + s // 2) % 2) * 2 + (core + s % 2) % 2
+
+    def h_peer(s):
+        return {"hidden": h_of(s)}
 
     def z_peer(k):
         return {"labels": (z + k) % 8}
@@ -85,7 +89,7 @@
         return {"frames": y * 2 + xx % 2, "hidden": (xx // 2) * 2 + (1 - core)}
 
     barrier = pltpu.get_barrier_semaphore()
-    greeted = [h_peer(k) for k in (1, 2, 3)] + [z_peer(k) for k in range(1, 8)]
+    greeted = [h_peer(s) for s in (1, 2, 3)] + [z_peer(k) for k in range(1, 8)]
     greeted += [f_peer(k) for k in range(1, 8)] + [x_peer(k) for k in (1, 3)]
     greeted += [z_other(k) for k in range(1, 8)] + [x_other(k) for k in (1, 3)]
     for device in greeted:
@@ -101,8 +105,9 @@
 
     prow = lax.broadcasted_iota(jnp.int32, (128, 128), 0)
     pcol = lax.broadcasted_iota(jnp.int32, (128, 128), 1)
-    pr = prow % 8
-    pframe = ((prow // 32) * 2 + pr // 4) * 16 + ((h + (prow // 8) % 4) % 4) * 4 + pr % 4
+    pslot = (prow // 8) % 4
+    pj = (prow // 32) * 8 + prow % 8
+    pframe = (pj // 4) * 16 + h_of(pslot) * 4 + pj % 4
     perm = (pcol == pframe).astype(F32).astype(BF16)
     tcol = jnp.zeros((16, 128), jnp.int32)
     trow = lax.broadcasted_iota(jnp.int32, (16, 128), 0)
@@ -124,53 +129,63 @@
     loads[4].wait()
     hidden = jnp.maximum(jnp.dot(feat_p, up[...], preferred_element_type=F32), 0.0).astype(BF16)
 
-    pl.semaphore_wait(barrier, len(greeted))
-    for k in (1, 2, 3):
-        send(msg.at[(h + k) % 4], msg_r.at[k - 1], msg_ss, msg_rs, h_peer(k))
-
     loads[5].wait()
     enc = jnp.dot(hidden, down[...], preferred_element_type=F32)
     for c in range(CH):
-        for k in range(4):
-            r = c * 32 + k * 8
-            part[c, k] = enc[r:r + 8, :]
-    for c in range(CH):
-        for k in (1, 2, 3):
-            send(part.at[c, k], part_r.at[c, k - 1], part_ss, part_rs.at[c], h_peer(k))
-
+        for s in range(4):
+            r = c * 32 + s * 8
+            part[c, s] = enc[r:r + 8, :]
     vocab_id = lax.broadcasted_iota(jnp.int32, (RB, 128), 1).astype(F32)
-    drain(msg_r, msg_rs)
-    for k in range(4):
-        src = msg.at[h] if k == 0 else msg_r.at[k - 1]
+
+    def labels_of(k):
+        if k:
+            drain(msg_r.at[k - 1], msg_rs.at[k - 1])
+        src = msg_r.at[k - 1] if k else msg.at[h]
         rows = slice(k * 16, k * 16 + 16)
         pred64[rows, :] = src[:, 0:JD]
         tail = src[:, JD:JD + 128]
         tg = jnp.broadcast_to(tail[:, 8:9], (16, 128))
         for n in range(8):
             hot[rows, n * 128:n * 128 + 128] = jnp.where(vocab_id == tg - float(n * 128), 1.0, 0.0)
-        for t in range(CH * FT):
-            r = t * LB + k * 16
+        for t in range(FR):
+            r = (k * FR + t) * 16
             at = (t // 4) * 16 + t % 4
             b = jnp.broadcast_to(tail[:, at:at + 1], (16, 128))
             l = jnp.broadcast_to(tail[:, at + 4:at + 5], (16, 128))
             wsum[r:r + 16, :] = b + l
             wblank[r:r + 16, :] = b
             wlabel[r:r + 16, :] = l
+
+    labels_of(0)
+    pl.semaphore_wait(barrier, len(greeted))
+    for s in (2, 3, 1):
+        send(msg.at[h_of(s)], msg_r.at[s - 1], msg_ss, msg_rs.at[s - 1], h_peer(s))
+    for c in range(CH):
+        for s in (2, 3, 1):
+            send(part.at[c, s], part_r.at[c, s - 1], part_ss, part_rs.at[c], h_peer(s))
+    for k in (1, 2, 3):
+        labels_of(k)
     loads[6].wait()
 
     def logits_of(c):
         drain(part_r.at[c], part_rs.at[c])
         enc8 = part[c, 0] + part_r[c, 0] + part_r[c, 1] + part_r[c, 2]
         for t in range(FT):
-            cells = jnp.tanh(pred64[...] + enc8[t:t + 1, :])
-            joint[c * CELLS + t * LB:c * CELLS + t * LB + LB, :] = cells.astype(BF16)
-        lg[c % 2] = jnp.dot(joint[c * CELLS:c * CELLS + CELLS, :], w[...], preferred_element_type=F32)
+            cells = jnp.tanh(pred64[...] + enc8[t:t + 1, :]).astype(BF16)
+            for k in range(4):
+                r = (k * FR + c * FT + t) * 16
+                joint[r:r + 16, :] = cells[k * 16:k * 16 + 16, :]
+        ends = [(k * FR + c * FT) * 16 for k in range(4)]
+        lhs = jnp.concatenate([joint[r:r + FT * 16, :] for r in ends], axis=0)
+        lg[c % 2] = jnp.dot(lhs, w[...], preferred_element_type=F32)
 
     def softmax_of(c):
         for i in range(CELLS // RB):
             rows = slice(i * RB, i * RB + RB)
-            cell = slice(c * CELLS + i * RB, c * CELLS + i * RB + RB)
-            label = slice((i * RB) % LB, (i * RB) % LB + RB)
+            block, t = i // FT, c * FT + i % FT
+            r = (block * FR + t) * 16
+            cell = slice(r, r + 16)
+            label = slice(block * 16, block * 16 + 16)
             tiles = [lg[c % 2, rows, n * 128:n * 128 + 128] for n in range(8)]
             m = tiles[0]
             for tile in tiles[1:]:
@@ -189,10 +204,10 @@
                 grad[cell, n * 128:n * 128 + 128] = g.astype(BF16)
 
     logits_of(0)
-    for c in range(1, CH):
+    for c in range(1, 4):
         logits_of(c)
         softmax_of(c - 1)
-    softmax_of(CH - 1)
+    softmax_of(3)
 
     def head_block(i):
         yy = (y + 1 + i) % 4
@@ -222,11 +237,11 @@
         hab[core, yy] = hab[core, yy] + h1ab[yy]
         for k in (1, 2, 3):
             at = pl.multiple_of(((x + k) % 4) * 8, 8)
-            send(hab.at[core, yy, 0, pl.ds(at, 8)], p1a.at[k - 1, yy], p1_ss.at[0], p1_rs.at[0], x_peer(k))
+            send(hab.at[core, yy, 0, pl.ds(at, 8)], p1a.at[yy, k - 1], p1_ss.at[0], p1a_rs.at[yy], x_peer(k))
 
         @pl.when(i < 3)
         def _():
-            send(hab.at[core, yy, 1], p1b.at[i], p1_ss.at[1], p1_rs.at[1], {"frames": yy * 2 + x_lo})
+            send(hab.at[core, yy, 1], p1b.at[i], p1_ss.at[1], p1b_rs, {"frames": yy * 2 + x_lo})
 
         @pl.when(core == 0)
         def _():
@@ -234,7 +249,36 @@
             hc[yy] = hc[yy] + h1c[yy]
             for k in range(1, 8):
                 at = pl.multiple_of(((z + k) % 8) * 4, 4)
-                send(hc.at[yy, pl.ds(at, 4)], p1c.at[k - 1, yy], p1_ss.at[2], p1_rs.at[2], z_peer(k))
+                send(hc.at[yy, pl.ds(at, 4)], p1c.at[yy, k - 1], p1_ss.at[2], p1c_rs.at[yy], z_peer(k))
+
+    own = pl.ds(pl.multiple_of(x * 8, 8), 8)
+    mine = pl.ds(pl.multiple_of(z * 4, 4), 4)
+
+    def second_a(i, away=True):
+        yy = (y + 1 + i) % 4
+        drain(p1a.at[yy], p1a_rs.at[yy])
+        a1[yy] = hab[core, yy, 0, own] + p1a[yy, 0] + p1a[yy, 1] + p1a[yy, 2]
+        if away:
+            send(a1.at[yy], p2a.at[i], p2_ss.at[0], p2_rs.at[0], {"frames": yy * 2 + x_lo})
+
+    def second_b():
+        drain(p1b, p1b_rs)
+        b1[...] = hab[core, y, 1] + p1b[0] + p1b[1] + p1b[2]
+        for k in (1, 2, 3):
+            at = pl.multiple_of(((x + k) % 4) * 8, 8)
+            send(b1.at[pl.ds(at, 8)], p2b.at[k - 1], p2_ss.at[1], p2_rs.at[1], x_peer(k))
+
+    def second_c(i, away=True):
+        @pl.when(core == 0)
+        def _():
+            yy = (y + 1 + i) % 4
+            drain(p1c.at[yy], p1c_rs.at[yy])
+            tot = hc[yy, mine]
+            for k in range(7):
+                tot = tot + p1c[yy, k]
+            c1[yy] = tot
+            if away:
+                send(c1.at[yy], p2c.at[i], p2_ss.at[2], p2_rs.at[2], {"frames": yy * 2 + x_lo})
 
     def head_step(i, carry):
         head_block(i)
@@ -247,82 +291,75 @@
 
     lax.fori_loop(0, 4, head_step, 0)
 
-    predp[...] = jnp.zeros_like(predp)
-
-    def backward(c, carry):
-        base = pl.multiple_of(c * CELLS, CELLS)
+    def backward(k, first=False, last=False):
+        r = k * FR * 16
         jg[...] = lax.dot_general(
-            grad[pl.ds(base, CELLS), :], w[...], (((1,), (1,)), ((), ())), preferred_element_type=F32
+            grad[r:r + FR * 16, :], w[...], (((1,), (1,)), ((), ())), preferred_element_type=F32
         )
         for n in range(5):
             cols = slice(n * 128, n * 128 + 128)
-            acc = predp[:, cols]
-            for t in range(FT):
-                cells = joint[pl.ds(pl.multiple_of(base + t * LB, LB), LB), cols].astype(F32)
-                tg = jg[t * LB:t * LB + LB, cols] * (1.0 - cells * cells)
+            acc = jnp.zeros((16, 128), F32)
+            for t in range(FR):
+                cells = joint[r + t * 16:r + t * 16 + 16, cols].astype(F32)
+                tg = jg[t * 16:t * 16 + 16, cols] * (1.0 - cells * cells)
                 acc = acc + tg
-                encp[c * 2 + t // 4, t % 4:t % 4 + 1, cols] = jnp.sum(tg, axis=0, keepdims=True)
-            predp[:, cols] = acc
-        return carry
-
-    backward(0, 0)
+                both = tg[0:8, :] + tg[8:16, :]
+                if not first:
+                    both = both + encacc[t, :, cols]
+                if last:
+                    encp[t // 4, t % 4:t % 4 + 1, cols] = jnp.sum(both, axis=0, keepdims=True)
+                else:
+                    encacc[t, :, cols] = both
+            predp[k * 16:k * 16 + 16, cols] = acc
+        if k:
+            send(predp.at[pl.ds(k * 16, 16)], predp_r.at[k - 1], predp_ss, predp_rs, h_peer(k))
+
+    backward(2, first=True)
     head_spread(3)
-    lax.fori_loop(1, CH, backward, 0)
+    backward(3)
+    second_a(0)
+    backward(1)
+    second_a(1)
+    second_c(0)
+    backward(0, last=True)
 
     for k in range(1, 8):
         send(encp.at[(z + k) % 8], encp_r.at[k - 1], encp_ss, encp_rs, z_peer(k))
-    for k in (1, 2, 3):
-        send(predp.at[pl.ds(k * 16, 16)], predp_r.at[k - 1], predp_ss, predp_rs, h_peer(4 - k))
-
-    drain(p1a, p1_rs.at[0])
-    own = pl.ds(pl.multiple_of(x * 8, 8), 8)
-    for yy in range(4):
-        a1[yy] = hab[core, yy, 0, own] + p1a[0, yy] + p1a[1, yy] + p1a[2, yy]
-    for k in (1, 2, 3):
-        send(a1.at[(y + k) % 4], p2a.at[k - 1], p2_ss.at[0], p2_rs.at[0], y_peer(k))
-    drain(p1b, p1_rs.at[1])
-    b1[...] = hab[core, y, 1] + p1b[0] + p1b[1] + p1b[2]
-    for k in (1, 2, 3):
-        at = pl.multiple_of(((x + k) % 4) * 8, 8)
-        send(b1.at[pl.ds(at, 8)], p2b.at[k - 1], p2_ss.at[1], p2_rs.at[1], x_peer(k))
-
-    @pl.when(core == 0)
-    def _():
-        drain(p1c, p1_rs.at[2])
-        mine = pl.ds(pl.multiple_of(z * 4, 4), 4)
-        for yy in range(4):
-            tot = hc[yy, mine]
-            for k in range(7):
-                tot = tot + p1c[k, yy]
-            c1[yy] = tot
-        for k in (1, 2, 3):
-            send(c1.at[(y + k) % 4], p2c.at[k - 1], p2_ss.at[2], p2_rs.at[2], y_peer(k))
-
+    second_a(2)
+    second_c(1)
+    second_b()
     drain(predp_r, predp_rs)
     predb[...] = predp[0:16, :] + predp_r[0] + predp_r[1] + predp_r[2]
     for k in range(1, 8):
         send(predb, predb_r.at[k - 1], predb_ss, predb_rs, f_peer(k))
+
+    second_c(2)
+    second_a(3, away=False)
+    second_c(3, away=False)
 
     drain(p2a, p2_rs.at[0])
     a2 = a1[y] + p2a[0] + p2a[1] + p2a[2]
     drain(p2b, p2_rs.at[1])
     b2 = b1[own] + p2b[0] + p2b[1] + p2b[2]
     for zz in range(8):
-        ab2[zz, 0] = a2[zz]
-        ab2[zz, 1] = b2[zz]
+        for n in range(2):
+            ab2[zz, n, 0] = a2[zz, n * 4:n * 4 + 4, :]
+            ab2[zz, n, 1] = b2[zz, n * 4:n * 4 + 4, :]
     for k in range(8):
-        send(ab2.at[(z + k) % 8], p3oth.at[k], p3_ss.at[1], p3_rs.at[1], z_other(k))
+        send(ab2.at[(z + k) % 8, 1 - core], p3oth.at[k], p3_ss.at[1], p3_rs.at[1], z_other(k))
         if k:
-            send(ab2.at[(z + k) % 8], p3own.at[k - 1], p3_ss.at[0], p3_rs.at[0], z_peer(k))
+            send(ab2.at[(z + k) % 8, core], p3own.at[k - 1], p3_ss.at[0], p3_rs.at[0], z_peer(k))
 
     @pl.when(core == 0)
     def _():
         drain(p2c, p2_rs.at[2])
-        c2[...] = c1[y] + p2c[0] + p2c[1] + p2c[2]
+        tot = c1[y] + p2c[0] + p2c[1] + p2c[2]
+        for n in range(2):
+            c2[:, n] = tot[:, n * 4:n * 4 + 4, :]
         for k in range(4):
-            send(c2.at[(x + k) % 4], p3d.at[k], p3_ss.at[3], p3_rs.at[3], x_other(k))
+            send(c2.at[(x + k) % 4, 1], p3d.at[k], p3_ss.at[3], p3_rs.at[3], x_other(k))
             if k:
-                send(c2.at[(x + k) % 4], p3c.at[k - 1], p3_ss.at[2], p3_rs.at[2], x_peer(k))
+                send(c2.at[(x + k) % 4, 0], p3c.at[k - 1], p3_ss.at[2], p3_rs.at[2], x_peer(k))
 
     drain(encp_r, encp_rs)
     tot = encp[z]
@@ -337,7 +374,7 @@
     pred_out[...] = tot
 
     drain(p3own, p3_rs.at[0])
-    tot = ab2[z]
+    tot = ab2[z, core]
     for k in range(7):
         tot = tot + p3own[k]
     fin[core, 0:2] = tot
@@ -350,7 +387,7 @@
     @pl.when(core == 0)
     def _():
         drain(p3c, p3_rs.at[2])
-        fin[0, 2] = c2[x] + p3c[0] + p3c[1] + p3c[2]
+        fin[0, 2] = c2[x, 0] + p3c[0] + p3c[1] + p3c[2]
 
     @pl.when(core == 1)
     def _():
@@ -358,9 +395,7 @@
         fin[0, 2] = p3d[0] + p3d[1] + p3d[2] + p3d[3]
 
     for n in range(5):
-        tile = fin[n // 3, n % 3]
-        mine = jnp.where(core == 0, tile[0:4, :], tile[4:8, :])
-        head_out[:, n * 128:n * 128 + 128] = mine
+        head_out[:, n * 128:n * 128 + 128] = fin[n // 3, n % 3]
 
     drain(msg_r, msg_ss)
     drain(part_r, part_ss)
@@ -399,21 +434,23 @@
     scratch = [
         V((128, 1024), BF16), V((1024, 1024), BF16), V((1024, JD), BF16), V((JD, VOCAB), BF16),
         V((16, JD), BF16), V((16, 128), F32), V((16, 128), F32), dma((7,)),
-        V((4, 16, JD + 128), F32), V((3, 16, JD + 128), F32), dma, dma,
+        V((4, 16, JD + 128), F32), V((3, 16, JD + 128), F32), dma, dma((3,)),
         V((CH, 4, 8, JD), F32), V((CH, 3, 8, JD), F32), dma, dma((CH,)),
         V((LB, JD), F32), V((2048, 128), F32), V((2048, 128), F32), V((2048, 128), F32), V((LB, VOCAB), F32),
+        V((FR, 8, JD), F32),
         V((2048, JD), BF16), V((2, CELLS, VOCAB), F32), V((2048, VOCAB), BF16), V((CELLS, JD), F32),
         V((8, 4, JD), F32), V((7, 4, JD), F32), dma, dma,
         V((LB, JD), F32), V((3, 16, JD), F32), dma, dma,
         V((16, JD), F32), V((7, 16, JD), F32), dma, dma,
         V((2, 4, 2, 32, 8, 128), F32), V((4, 32, 8, 128), F32),
         V((4, 2, 32, 8, 128), F32), V((4, 32, 8, 128), F32), dma, dma((4,)), dma, dma((4,)),
-        V((3, 4, 8, 8, 128), F32), V((3, 32, 8, 128), F32), V((7, 4, 4, 8, 128), F32), dma((3,)), dma((3,)),
+        V((4, 3, 8, 8, 128), F32), V((3, 32, 8, 128), F32), V((4, 7, 4, 8, 128), F32),
+        dma((3,)), dma((4,)), dma, dma((4,)),
         V((4, 8, 8, 128), F32), V((32, 8, 128), F32), V((4, 4, 8, 128), F32),
         V((3, 8, 8, 128), F32), V((3, 8, 8, 128), F32), V((3, 4, 8, 128), F32), dma((3,)), dma((3,)),
-        V((8, 2, 8, 128), F32), V((4, 8, 128), F32), V((7, 2, 8, 128), F32), V((8, 2, 8, 128), F32),
-        V((3, 8, 128), F32), V((4, 8, 128), F32), dma((4,)), dma((4,)),
-        V((2, 3, 8, 128), F32),
+        V((8, 2, 2, 4, 128), F32), V((4, 2, 4, 128), F32), V((7, 2, 4, 128), F32), V((8, 2, 4, 128), F32),
+        V((3, 4, 128), F32), V((4, 4, 128), F32), dma((4,)), dma((4,)),
+        V((2, 3, 4, 128), F32),
     ]
     hbm = pl.BlockSpec(memory_space=pl.ANY)
     vmem = pl.BlockSpec(memory_space=pltpu.VMEM)

time: 46.5 us -> 46.4 us (level)
  no operation moved by 1% of the time
where the time goes in v3:
time: 46.4 us; the launch traced here: 46.1 us
  Pallas kernels  45.5 us (98%)
  between operations  0.64 us (1%)
    pallas_call x1, Pallas kernels, on_device(): pl.pallas_call(kernel, out_shape=shapes, in_specs=[hbm] * 7 + [smem], out...  44.1 us
    pallas_call x1, Pallas kernels, on_device(): pl.pallas_call(hand_on, out_shape=shapes, in_specs=[vmem] * 3, out_specs=...  1.4 us

profile of v3, /device:TPU:1, one launch (start us, length us, event | category | flops | bytes accessed | tf_op | source)
XLA Modules:
  0.0 46.1 jit_solution(6285823096343423490)
XLA Ops:
  0.6 44.1 %shard_map.103 = (f32[4,640]{1,0:T(4,128)}, f32[16,640]{1,0:T(8,128)}, f32[4,640]{1,0:T(4,128)}) custom-call(bf16[128,1024]{1,0:T(8,128)(2,1)} %feat_hbm.1, bf16[1024,1024]{1,0:T(8,128)(2,1)} %up_hbm.1, bf16[1024,640]{1,0:T(8,128)(2,1)} %down_hbm.1, bf16[16,640]{1,0:T(8,128)(2,1)} %pred_hbm.1, bf16[640,1024]{1,0:T(8,128)(2,1)} %w_hbm.1, f32[16,128]{1,0:T(8,128)} %bitcast.2, ...), custom_call_target="tpu_custom_call" | custom-call | tf_op jit(solution)/shard_map/pallas_call | solution.py:463
  44.7 1.4 %shard_map.104 = (f32[4,640]{1,0:T(4,128)}, f32[16,640]{1,0:T(8,128)}, f32[4,640]{1,0:T(4,128)}) custom-call(f32[4,640]{1,0:T(4,128)} %get-tuple-element.6.enc_in, f32[16,640]{1,0:T(8,128)} %get-tuple-element.7.pred_in, f32[4,640]{1,0:T(4,128)} %get-tuple-element.8.head_in), custom_call_target="tpu_custom_call" | custom-call | tf_op jit(solution)/shard_map/pallas_call | solution.py:473

commit v4 on v3

--- a/solution.py
+++ b/solution.py
@@ -40,12 +40,14 @@
     enc_out, pred_out, head_out,
     feat, up, down, w, pred_in, blank_in, label_in, load_sem,
     msg, msg_r, msg_ss, msg_rs,
+    tails, tails_r, tails_ss, tails_rs,
     part, part_r, part_ss, part_rs,
     pred64, wsum, wblank, wlabel, hot, encacc,
     joint, lg, grad, jg,
     encp, encp_r, encp_ss, encp_rs,
     predp, predp_r, predp_ss, predp_rs,
     predb, predb_r, predb_ss, predb_rs,
+    predx_r, predy, predx_ss, predx_rs,
     hab, hc, h1ab, h1c, h1ab_ss, h1ab_rs, h1c_ss, h1c_rs,
     p1a, p1b, p1c, p1_ss, p1a_rs, p1b_rs, p1c_rs,
     a1, b1, c1, p2a, p2b, p2c, p2_ss, p2_rs,
@@ -119,15 +121,18 @@
         loads[n].wait()
     feat_p = jnp.dot(perm, feat[...], preferred_element_type=F32).astype(BF16)
 
-    pred_wide = pred_in[...].astype(F32)
+    msg[...] = pred_in[...].astype(F32)
     for d in range(4):
-        msg[d, :, 0:JD] = pred_wide
         b = pltpu.roll(blank_in[...], (128 - 4 * d) % 128, 1)
         l = pltpu.roll(label_in[...], (132 - 4 * d) % 128, 1)
-        msg[d, :, JD:JD + 128] = jnp.where(lane < 4, b, jnp.where(lane < 8, l, tfloat))
+        tails[d] = jnp.where(lane < 4, b, jnp.where(lane < 8, l, tfloat))
 
     loads[4].wait()
     hidden = jnp.maximum(jnp.dot(feat_p, up[...], preferred_element_type=F32), 0.0).astype(BF16)
+
+    pl.semaphore_wait(barrier, len(greeted))
+    for s in (2, 1):
+        send(msg, msg_r.at[s - 1], msg_ss, msg_rs.at[s - 1], h_peer(s))
 
     loads[5].wait()
     enc = jnp.dot(hidden, down[...], preferred_element_type=F32)
@@ -135,15 +140,24 @@
         for s in range(4):
             r = c * 32 + s * 8
             part[c, s] = enc[r:r + 8, :]
+    for c in range(CH):
+        for s in (2, 3, 1):
+            send(part.at[c, s], part_r.at[c, s - 1], part_ss, part_rs.at[c], h_peer(s))
+        if c == 0:
+            for s in (2, 3, 1):
+                send(tails.at[h_of(s)], tails_r.at[s - 1], tails_ss, tails_rs.at[s - 1], h_peer(s))
+
     vocab_id = lax.broadcasted_iota(jnp.int32, (RB, 128), 1).astype(F32)
 
     def labels_of(k):
         if k:
-            drain(msg_r.at[k - 1], msg_rs.at[k - 1])
-        src = msg_r.at[k - 1] if k else msg.at[h]
+            drain(tails_r.at[k - 1], tails_rs.at[k - 1])
+            if k != 2:
+                drain(msg_r.at[k - 1], msg_rs.at[k - 1])
+        src = msg_r.at[k - 1] if k else msg
         rows = slice(k * 16, k * 16 + 16)
-        pred64[rows, :] = src[:, 0:JD]
-        tail = src[:, JD:JD + 128]
+        pred64[rows, :] = src[...]
+        tail = tails_r[k - 1] if k else tails[h]
         tg = jnp.broadcast_to(tail[:, 8:9], (16, 128))
         for n in range(8):
             hot[rows, n * 128:n * 128 + 128] = jnp.where(vocab_id == tg - float(n * 128), 1.0, 0.0)
@@ -157,12 +171,8 @@
             wlabel[r:r + 16, :] = l
 
     labels_of(0)
-    pl.semaphore_wait(barrier, len(greeted))
-    for s in (2, 3, 1):
-        send(msg.at[h_of(s)], msg_r.at[s - 1], msg_ss, msg_rs.at[s - 1], h_peer(s))
-    for c in range(CH):
-        for s in (2, 3, 1):
-            send(part.at[c, s], part_r.at[c, s - 1], part_ss, part_rs.at[c], h_peer(s))
+    drain(msg_r.at[1], msg_rs.at[1])
+    send(msg_r.at[1], msg_r.at[2], msg_ss, msg_rs.at[2], h_peer(1))
     for k in (1, 2, 3):
         labels_of(k)
     loads[6].wait()
@@ -330,12 +340,16 @@
     second_b()
     drain(predp_r, predp_rs)
     predb[...] = predp[0:16, :] + predp_r[0] + predp_r[1] + predp_r[2]
-    for k in range(1, 8):
-        send(predb, predb_r.at[k - 1], predb_ss, predb_rs, f_peer(k))
+    send(predb, predx_r, predx_ss, predx_rs, {"frames": y * 2 + 1 - x_lo})
 
     second_c(2)
     second_a(3, away=False)
     second_c(3, away=False)
+
+    drain(predx_r, predx_rs)
+    predy[...] = predb[...] + predx_r[...]
+    for k in (1, 2, 3):
+        send(predy, predb_r.at[k - 1], predb_ss, predb_rs, y_peer(k))
 
     drain(p2a, p2_rs.at[0])
     a2 = a1[y] + p2a[0] + p2a[1] + p2a[2]
@@ -368,10 +382,7 @@
     enc_out[...] = tot
 
     drain(predb_r, predb_rs)
-    tot = predb[...]
-    for k in range(7):
-        tot = tot + predb_r[k]
-    pred_out[...] = tot
+    pred_out[...] = predy[...] + predb_r[0] + predb_r[1] + predb_r[2]
 
     drain(p3own, p3_rs.at[0])
     tot = ab2[z, core]
@@ -398,10 +409,12 @@
         head_out[:, n * 128:n * 128 + 128] = fin[n // 3, n % 3]
 
     drain(msg_r, msg_ss)
+    drain(tails_r, tails_ss)
     drain(part_r, part_ss)
     drain(encp_r, encp_ss)
     drain(predp_r, predp_ss)
     drain(predb_r, predb_ss)
+    drain(predx_r, predx_ss)
     drain(h1ab, h1ab_ss)
     drain(p1a, p1_ss.at[0])
     drain(p1b, p1_ss.at[1])
@@ -434,14 +447,16 @@
     scratch = [
         V((128, 1024), BF16), V((1024, 1024), BF16), V((1024, JD), BF16), V((JD, VOCAB), BF16),
         V((16, JD), BF16), V((16, 128), F32), V((16, 128), F32), dma((7,)),
-        V((4, 16, JD + 128), F32), V((3, 16, JD + 128), F32), dma, dma((3,)),
+        V((16, JD), F32), V((3, 16, JD), F32), dma, dma((3,)),
+        V((4, 16, 128), F32), V((3, 16, 128), F32), dma, dma((3,)),
         V((CH, 4, 8, JD), F32), V((CH, 3, 8, JD), F32), dma, dma((CH,)),
         V((LB, JD), F32), V((2048, 128), F32), V((2048, 128), F32), V((2048, 128), F32), V((LB, VOCAB), F32),
         V((FR, 8, JD), F32),
         V((2048, JD), BF16), V((2, CELLS, VOCAB), F32), V((2048, VOCAB), BF16), V((CELLS, JD), F32),
         V((8, 4, JD), F32), V((7, 4, JD), F32), dma, dma,
         V((LB, JD), F32), V((3, 16, JD), F32), dma, dma,
-        V((16, JD), F32), V((7, 16, JD), F32), dma, dma,
+        V((16, JD), F32), V((3, 16, JD), F32), dma, dma,
+        V((16, JD), F32), V((16, JD), F32), dma, dma,
         V((2, 4, 2, 32, 8, 128), F32), V((4, 32, 8, 128), F32),
         V((4, 2, 32, 8, 128), F32), V((4, 32, 8, 128), F32), dma, dma((4,)), dma, dma((4,)),
         V((4, 3, 8, 8, 128), F32), V((3, 32, 8, 128), F32), V((4, 7, 4, 8, 128), F32),

time: 46.4 us -> 45.7 us (0.985)
  Pallas kernels: 45.5 us -> 44.9 us
    pallas_call x1, Pallas kernels: 44.1 us -> 43.5 us  [on_device(): pl.pallas_call(kernel, out_shape=shapes, in_specs=[hbm] * 7 + [smem], out...]
where the time goes in v4:
time: 45.7 us; the launch traced here: 45.6 us
  Pallas kernels  44.9 us (98%)
  between operations  0.64 us (1%)
    pallas_call x1, Pallas kernels, on_device(): pl.pallas_call(kernel, out_shape=shapes, in_specs=[hbm] * 7 + [smem], out...  43.5 us
    pallas_call x1, Pallas kernels, on_device(): pl.pallas_call(hand_on, out_shape=shapes, in_specs=[vmem] * 3, out_specs=...  1.4 us

profile of v4, /device:TPU:1, one launch (start us, length us, event | category | flops | bytes accessed | tf_op | source)
XLA Modules:
  0.0 45.6 jit_solution(14418004486593520775)
XLA Ops:
  0.6 43.5 %shard_map.103 = (f32[4,640]{1,0:T(4,128)}, f32[16,640]{1,0:T(8,128)}, f32[4,640]{1,0:T(4,128)}) custom-call(bf16[128,1024]{1,0:T(8,128)(2,1)} %feat_hbm.1, bf16[1024,1024]{1,0:T(8,128)(2,1)} %up_hbm.1, bf16[1024,640]{1,0:T(8,128)(2,1)} %down_hbm.1, bf16[16,640]{1,0:T(8,128)(2,1)} %pred_hbm.1, bf16[640,1024]{1,0:T(8,128)(2,1)} %w_hbm.1, f32[16,128]{1,0:T(8,128)} %bitcast.2, ...), custom_call_target="tpu_custom_call" | custom-call | tf_op jit(solution)/shard_map/pallas_call | solution.py:478
  44.2 1.4 %shard_map.104 = (f32[4,640]{1,0:T(4,128)}, f32[16,640]{1,0:T(8,128)}, f32[4,640]{1,0:T(4,128)}) custom-call(f32[4,640]{1,0:T(4,128)} %get-tuple-element.6.enc_in, f32[16,640]{1,0:T(8,128)} %get-tuple-element.7.pred_in, f32[4,640]{1,0:T(4,128)} %get-tuple-element.8.head_in), custom_call_target="tpu_custom_call" | custom-call | tf_op jit(solution)/shard_map/pallas_call | solution.py:488

commit v5 on v4

--- a/solution.py
+++ b/solution.py
@@ -51,7 +51,7 @@
     hab, hc, h1ab, h1c, h1ab_ss, h1ab_rs, h1c_ss, h1c_rs,
     p1a, p1b, p1c, p1_ss, p1a_rs, p1b_rs, p1c_rs,
     a1, b1, c1, p2a, p2b, p2c, p2_ss, p2_rs,
-    ab2, c2, p3own, p3oth, p3c, p3d, p3_ss, p3_rs,
+    ab2, c2, p3own, p3oth, p3c, p3d, p3_ss, p3_rs, p3o_rs,
     fin,
 ):
     f = lax.axis_index("frames")
@@ -77,9 +77,6 @@
         xx = (x + k) % 4
         return {"frames": y * 2 + xx % 2, "hidden": (xx // 2) * 2 + core}
 
-    def f_peer(k):
-        return {"frames": (f + k) % 8}
-
     other = x_hi * 2 + (1 - core)
     partner = {"hidden": other}
 
@@ -92,7 +89,7 @@
 
     barrier = pltpu.get_barrier_semaphore()
     greeted = [h_peer(s) for s in (1, 2, 3)] + [z_peer(k) for k in range(1, 8)]
-    greeted += [f_peer(k) for k in range(1, 8)] + [x_peer(k) for k in (1, 3)]
+    greeted += [y_peer(k) for k in (1, 2, 3)] + [x_peer(k) for k in (1, 3)]
     greeted += [z_other(k) for k in range(1, 8)] + [x_other(k) for k in (1, 3)]
     for device in greeted:
         pl.semaphore_signal(barrier, inc=1, device_id=device, device_id_type=pl.DeviceIdType.MESH)
@@ -111,24 +108,26 @@
     pj = (prow // 32) * 8 + prow % 8
     pframe = (pj // 4) * 16 + h_of(pslot) * 4 + pj % 4
     perm = (pcol == pframe).astype(F32).astype(BF16)
-    tcol = jnp.zeros((16, 128), jnp.int32)
-    trow = lax.broadcasted_iota(jnp.int32, (16, 128), 0)
-    for i in range(16):
-        tcol = jnp.where(trow == i, targets[i], tcol)
-    tfloat = tcol.astype(F32)
-    lane = lax.broadcasted_iota(jnp.int32, (16, 128), 1) % 16
     for n in range(4):
         loads[n].wait()
     feat_p = jnp.dot(perm, feat[...], preferred_element_type=F32).astype(BF16)
 
     msg[...] = pred_in[...].astype(F32)
-    for d in range(4):
-        b = pltpu.roll(blank_in[...], (128 - 4 * d) % 128, 1)
-        l = pltpu.roll(label_in[...], (132 - 4 * d) % 128, 1)
-        tails[d] = jnp.where(lane < 4, b, jnp.where(lane < 8, l, tfloat))
-
     loads[4].wait()
     hidden = jnp.maximum(jnp.dot(feat_p, up[...], preferred_element_type=F32), 0.0).astype(BF16)
+
+    def build_tails():
+        tcol = jnp.zeros((16, 128), jnp.int32)
+        trow = lax.broadcasted_iota(jnp.int32, (16, 128), 0)
+        for i in range(16):
+            tcol = jnp.where(trow == i, targets[i], tcol)
+        tfloat = tcol.astype(F32)
+        lane = lax.broadcasted_iota(jnp.int32, (16, 128), 1) % 16
+
+        for d in range(4):
+            b = pltpu.roll(blank_in[...], (128 - 4 * d) % 128, 1)
+            l = pltpu.roll(label_in[...], (132 - 4 * d) % 128, 1)
+            tails[d] = jnp.where(lane < 4, b, jnp.where(lane < 8, l, tfloat))
 
     pl.semaphore_wait(barrier, len(greeted))
     for s in (2, 1):
@@ -144,6 +143,7 @@
         for s in (2, 3, 1):
             send(part.at[c, s], part_r.at[c, s - 1], part_ss, part_rs.at[c], h_peer(s))
         if c == 0:
+            build_tails()
             for s in (2, 3, 1):
                 send(tails.at[h_of(s)], tails_r.at[s - 1], tails_ss, tails_rs.at[s - 1], h_peer(s))
 
@@ -351,19 +351,19 @@
     for k in (1, 2, 3):
         send(predy, predb_r.at[k - 1], predb_ss, predb_rs, y_peer(k))
 
+    def third(n, tot):
+        for zz in range(8):
+            for half in range(2):
+                ab2[n, zz, half] = tot[zz, half * 4:half * 4 + 4, :]
+        for k in range(8):
+            send(ab2.at[n, (z + k) % 8, 1 - core], p3oth.at[n, k], p3_ss.at[1], p3o_rs.at[n], z_other(k))
+            if k:
+                send(ab2.at[n, (z + k) % 8, core], p3own.at[n, k - 1], p3_ss.at[0], p3_rs.at[n], z_peer(k))
+
     drain(p2a, p2_rs.at[0])
-    a2 = a1[y] + p2a[0] + p2a[1] + p2a[2]
+    third(0, a1[y] + p2a[0] + p2a[1] + p2a[2])
     drain(p2b, p2_rs.at[1])
-    b2 = b1[own] + p2b[0] + p2b[1] + p2b[2]
-    for zz in range(8):
-        for n in range(2):
-            ab2[zz, n, 0] = a2[zz, n * 4:n * 4 + 4, :]
-            ab2[zz, n, 1] = b2[zz, n * 4:n * 4 + 4, :]
-    for k in range(8):
-        send(ab2.at[(z + k) % 8, 1 - core], p3oth.at[k], p3_ss.at[1], p3_rs.at[1], z_other(k))
-        if k:
-            send(ab2.at[(z + k) % 8, core], p3own.at[k - 1], p3_ss.at[0], p3_rs.at[0], z_peer(k))
-
+    third(1, b1[own] + p2b[0] + p2b[1] + p2b[2])
     @pl.when(core == 0)
     def _():
         drain(p2c, p2_rs.at[2])
@@ -384,16 +384,17 @@
     drain(predb_r, predb_rs)
     pred_out[...] = predy[...] + predb_r[0] + predb_r[1] + predb_r[2]
 
-    drain(p3own, p3_rs.at[0])
-    tot = ab2[z, core]
-    for k in range(7):
-        tot = tot + p3own[k]
-    fin[core, 0:2] = tot
-    drain(p3oth, p3_rs.at[1])
-    tot = p3oth[0]
-    for k in range(1, 8):
-        tot = tot + p3oth[k]
-    fin[1 - core, 0:2] = tot
+    for n in range(2):
+        drain(p3own.at[n], p3_rs.at[n])
+        tot = ab2[n, z, core]
+        for k in range(7):
+            tot = tot + p3own[n, k]
+        fin[core, n] = tot
+        drain(p3oth.at[n], p3o_rs.at[n])
+        tot = p3oth[n, 0]
+        for k in range(1, 8):
+            tot = tot + p3oth[n, k]
+        fin[1 - core, n] = tot
 
     @pl.when(core == 0)
     def _():
@@ -463,8 +464,8 @@
         dma((3,)), dma((4,)), dma, dma((4,)),
         V((4, 8, 8, 128), F32), V((32, 8, 128), F32), V((4, 4, 8, 128), F32),
         V((3, 8, 8, 128), F32), V((3, 8, 8, 128), F32), V((3, 4, 8, 128), F32), dma((3,)), dma((3,)),
-        V((8, 2, 2, 4, 128), F32), V((4, 2, 4, 128), F32), V((7, 2, 4, 128), F32), V((8, 2, 4, 128), F32),
-        V((3, 4, 128), F32), V((4, 4, 128), F32), dma((4,)), dma((4,)),
+        V((2, 8, 2, 4, 128), F32), V((4, 2, 4, 128), F32), V((2, 7, 4, 128), F32), V((2, 8, 4, 128), F32),
+        V((3, 4, 128), F32), V((4, 4, 128), F32), dma((4,)), dma((4,)), dma((2,)),
         V((2, 3, 4, 128), F32),
     ]
     hbm = pl.BlockSpec(memory_space=pl.ANY)

time: 45.7 us -> 45.9 us (level)
  no operation moved by 1% of the time
where the time goes in v5:
time: 45.9 us; the launch traced here: 45.8 us
  Pallas kernels  45.1 us (98%)
  between operations  0.64 us (1%)
    pallas_call x1, Pallas kernels, on_device(): pl.pallas_call(kernel, out_shape=shapes, in_specs=[hbm] * 7 + [smem], out...  43.7 us
    pallas_call x1, Pallas kernels, on_device(): pl.pallas_call(hand_on, out_shape=shapes, in_specs=[vmem] * 3, out_specs=...  1.4 us

profile of v5, /device:TPU:1, one launch (start us, length us, event | category | flops | bytes accessed | tf_op | source)
XLA Modules:
  0.0 45.8 jit_solution(5694497426364972053)
XLA Ops:
  0.6 43.7 %shard_map.103 = (f32[4,640]{1,0:T(4,128)}, f32[16,640]{1,0:T(8,128)}, f32[4,640]{1,0:T(4,128)}) custom-call(bf16[128,1024]{1,0:T(8,128)(2,1)} %feat_hbm.1, bf16[1024,1024]{1,0:T(8,128)(2,1)} %up_hbm.1, bf16[1024,640]{1,0:T(8,128)(2,1)} %down_hbm.1, bf16[16,640]{1,0:T(8,128)(2,1)} %pred_hbm.1, bf16[640,1024]{1,0:T(8,128)(2,1)} %w_hbm.1, f32[16,128]{1,0:T(8,128)} %bitcast.2, ...), custom_call_target="tpu_custom_call" | custom-call | tf_op jit(solution)/shard_map/pallas_call | solution.py:479
  44.4 1.4 %shard_map.104 = (f32[4,640]{1,0:T(4,128)}, f32[16,640]{1,0:T(8,128)}, f32[4,640]{1,0:T(4,128)}) custom-call(f32[4,640]{1,0:T(4,128)} %get-tuple-element.6.enc_in, f32[16,640]{1,0:T(8,128)} %get-tuple-element.7.pred_in, f32[4,640]{1,0:T(4,128)} %get-tuple-element.8.head_in), custom_call_target="tpu_custom_call" | custom-call | tf_op jit(solution)/shard_map/pallas_call | solution.py:489
